TPU v7x, 128 devices: a whole 4x4x4 slice. The times are simulated.
128 devices in a mesh: dp: 16 (over x, y), mp: 8 (over z, core).
Axes of the slice: x: 4, y: 4, z: 4, core: 2. Of those that a mesh axis runs over, the one named last changes fastest.
Arguments:
- patches: bfloat16 [4096, 6144], P('dp', 'mp'), may hold values from -6 to 6
- dest_group: int32 [4096], P('dp'), may hold values from 0 to 15, as said below
- dest_row: int32 [4096], P('dp'), may hold values from 0 to 255, as said below
- segment: int32 [4096], P('dp'), may hold values from 0 to 31, as said below
- ln_gain: float32 [6144], replicated, may hold values from 0.1 to 1.9
- w_qkv: bfloat16 [6144, 3, 3072], P(None, None, 'mp'), may hold values from -0.078125 to 0.078125
- qk_gain: float32 [2, 128], replicated, may hold values from 0.1 to 1.9
- w_out: bfloat16 [6144, 3072], P(None, 'mp'), may hold values from -0.4375 to 0.4375
- cotangent: bfloat16 [4096, 6144], P('dp', 'mp'), may hold values from -6 to 6
Outputs:
- output: bfloat16 [4096, 6144], P('dp', 'mp')
- input_grad: bfloat16 [4096, 6144], P('dp', 'mp')
- qkv_grad: bfloat16 [6144, 3, 3072], P('dp', None, 'mp')
- out_grad: bfloat16 [6144, 3072], P('dp', 'mp')
Inputs may be any that keep to these rules, and one draw needn't show every extreme that they name: The pairs (dest_group, dest_row) of all rows name every row of every group exactly once. The rows of one group send at most 32 rows to any one group, and in every draw some group sends exactly 32 rows to some group. `dest_row`: see dest_group. `segment`: rows of one group with equal numbers are one image and stand in consecutive rows; numbers lie between 0 and 31.
All inputs are finite; a program needn't handle non-finite values.
Results may differ from a plain program's by a relative error of at most 0.024.
Values may be sent and summed in bfloat16 or wider, within the bound.
A program may use at most 192 MiB of HBM per device.

v0:
```python
import math

import jax
import jax.numpy as jnp
from jax import lax
from jax.sharding import PartitionSpec as P

DH = 128


def norm_heads(values, gain):
    center = values - jnp.mean(values, -1, keepdims=True)
    variance = jnp.mean(center * center, -1, keepdims=True)
    return center * lax.rsqrt(variance + 1e-06) * gain


def attend(projected, image_ids, qk_gain):
    row_count = projected.shape[0]
    head_count = projected.shape[2] // DH
    split_heads = projected.reshape(row_count, 3, head_count, DH)
    queries = norm_heads(split_heads[:, 0], qk_gain[0]).astype(jnp.bfloat16)
    keys_normed = norm_heads(split_heads[:, 1], qk_gain[1]).astype(jnp.bfloat16)
    values_bf = split_heads[:, 2].astype(jnp.bfloat16)
    scores = jnp.einsum(
        "qhd,khd->hqk", queries, keys_normed, preferred_element_type=jnp.float32
    ) * DH ** (-0.5)
    same_image = image_ids[:, None] == image_ids[None, :]
    raised = jnp.where(same_image[None], jnp.exp(scores), 0.0)
    weights = (raised / jnp.sum(raised, -1, keepdims=True)).astype(jnp.bfloat16)
    mixed = jnp.einsum("hqk,khd->qhd", weights, values_bf, preferred_element_type=jnp.float32)
    return mixed.reshape(row_count, head_count * DH).astype(jnp.bfloat16)


def contract_rows(left, right):
    return lax.dot_general(
        left, right, (((0,), (0,)), ((), ())), preferred_element_type=jnp.float32
    )


def contract_cols(left, right):
    return lax.dot_general(
        left, right, (((1,), (1,)), ((), ())), preferred_element_type=jnp.float32
    )


def shards(patches, dest_group, dest_row, segment, ln_gain, w_qkv, qk_gain, w_out, cotangent):
    group_rows, part_width = patches.shape
    groups = lax.axis_size("dp")
    slot_size = 2 * group_rows // groups
    full_width, local_width = w_out.shape
    member = (dest_group[:, None] == jnp.arange(groups, dtype=jnp.int32)[None, :]).astype(jnp.int32)
    rank_within = jnp.sum((jnp.cumsum(member, 0) - 1) * member, 1)
    place = dest_group * slot_size + rank_within
    outbox = jnp.zeros((groups * slot_size, part_width), patches.dtype).at[place].set(patches)
    address = jnp.full((groups * slot_size,), group_rows, jnp.int32).at[place].set(dest_row)
    inbox, arrived_at = (
        lax.all_to_all(
            outbox.reshape(groups, slot_size, part_width),
            "dp",
            split_axis=0,
            concat_axis=0,
            tiled=True,
        ),
        lax.all_to_all(
            address.reshape(groups, slot_size), "dp", split_axis=0, concat_axis=0, tiled=True
        ),
    )
    packed = (
        jnp.zeros((group_rows, part_width), patches.dtype)
        .at[arrived_at.reshape(-1)]
        .set(inbox.reshape(-1, part_width), mode="drop")
    )
    whole_rows, whole_cot = (
        lax.all_gather(packed, "mp", axis=1, tiled=True),
        lax.all_gather(cotangent, "mp", axis=1, tiled=True),
    )
    wide = whole_rows.astype(jnp.float32)
    center = wide - jnp.mean(wide, -1, keepdims=True)
    rstd = lax.rsqrt(jnp.mean(center * center, -1, keepdims=True) + 1e-06)
    unit_rows = center * rstd
    normed = (unit_rows * ln_gain).astype(jnp.bfloat16)
    w_flat = w_qkv.reshape(full_width, 3 * local_width)
    projected = jnp.dot(normed, w_flat, preferred_element_type=jnp.float32).reshape(
        group_rows, 3, local_width
    )
    heads_out, backward = jax.vjp(lambda values: attend(values, segment, qk_gain), projected)
    attn = lax.psum_scatter(
        contract_cols(heads_out, w_out).astype(jnp.bfloat16), "mp", scatter_dimension=1, tiled=True
    ).astype(jnp.float32)
    output = (packed.astype(jnp.float32) + attn).astype(jnp.bfloat16)
    d_heads = jnp.dot(whole_cot, w_out, preferred_element_type=jnp.float32).astype(jnp.bfloat16)
    (d_projected,) = backward(d_heads)
    d_proj_bf = d_projected.astype(jnp.bfloat16).reshape(group_rows, 3 * local_width)
    d_part = contract_cols(d_proj_bf, w_flat)
    my_index = lax.axis_index("mp")
    d_normed = lax.psum(d_part.astype(jnp.bfloat16), "mp").astype(jnp.float32)
    d_unit = d_normed * ln_gain
    d_full = rstd * (
        d_unit
        - jnp.mean(d_unit, -1, keepdims=True)
        - unit_rows * jnp.mean(d_unit * unit_rows, -1, keepdims=True)
    )
    d_input = lax.dynamic_slice_in_dim(d_full, my_index * part_width, part_width, 1)
    input_grad = (cotangent.astype(jnp.float32) + d_input).astype(jnp.bfloat16)
    sum_qkv, sum_out = (
        lax.psum_scatter(
            contract_rows(normed, d_proj_bf).astype(jnp.bfloat16),
            "dp",
            scatter_dimension=0,
            tiled=True,
        ).astype(jnp.float32),
        lax.psum_scatter(
            contract_rows(whole_cot, heads_out).astype(jnp.bfloat16),
            "dp",
            scatter_dimension=0,
            tiled=True,
        ).astype(jnp.float32),
    )
    scale_grad = 1.0 / math.sqrt(group_rows * groups)
    qkv_grad = (sum_qkv * scale_grad).reshape(-1, 3, local_width).astype(jnp.bfloat16)
    out_grad = (sum_out * scale_grad).astype(jnp.bfloat16)
    return (output, input_grad, qkv_grad, out_grad)


def solution(mesh):
    placed = (
        P("dp", "mp"),
        P("dp"),
        P("dp"),
        P("dp"),
        P(),
        P(None, None, "mp"),
        P(),
        P(None, "mp"),
        P("dp", "mp"),
    )
    return jax.shard_map(
        shards,
        mesh=mesh,
        in_specs=placed,
        out_specs=(P("dp", "mp"), P("dp", "mp"), P("dp", None, "mp"), P("dp", "mp")),
        check_vma=False,
    )
```

profile of v0, /device:TPU:1, one launch (start us, length us, event | category | flops | bytes accessed | tf_op | source)
XLA Modules:
  0.0 402.0 jit_solution(2269803845035048360)
XLA Ops:
  7.2 0.7 all-gather.5.cloned.1.call-update
  7.9 0.7 fusion.32
  8.6 0.6 reduce-window.6
  9.4 0.8 fusion.31
  10.2 0.7 compare_select_fusion.1
  10.8 1.6 scatter_custom_fusion
  12.4 0.7 all_to_all.9
  13.1 7.6 %all-to-all-start = ((s32[16,1,32]{2,1,0:T(1,128)}), s32[16,1,32]{2,1,0:T(1,128)S(1)}, u32[]{:S(2)}, u32[]{:S(2)}) async-start(s32[16,1,32]{2,1,0:T(1,128)} %all_to_all.9), calls=%async_computation | async-start | bytes 16384 | tf_op jit(solution)/shard_map/all_to_all | solution.py:64
  20.7 3.1 scatter_custom_fusion.1
  23.7 3.3 all-to-all-done
  27.0 3.6 all-to-all-start.1
  30.7 0.5 broadcast.243
  31.2 0.7 reduce.7
  32.0 10.6 %all-to-all-done.1 = bf16[16,32,768]{2,1,0:T(8,128)(2,1)S(1)} async-done(((bf16[16,32,768]{2,1,0:T(8,128)(2,1)}), bf16[16,32,768]{2,1,0:T(8,128)(2,1)S(1)}, u32[]{:S(2)}, u32[]{:S(2)}) %all-to-all-start.1) | async-done | bytes 786464 | tf_op jit(solution)/shard_map/all_to_all | solution.py:57
  42.6 3.3 scatter_custom_fusion.2
  45.9 0.2 all-reduce.5.cloned.1.call-start
  46.2 18.8 %copy.39 = bf16[6144,3,384]{0,2,1:T(8,128)(2,1)} copy(bf16[6144,3,384]{2,0,1:T(8,128)(2,1)} %param.14) | data formatting | bytes 28311552 | tf_op args[5]
  65.1 5.2 %convolution_convert_fusion.5 = bf16[256,384]{1,0:T(8,128)(2,1)S(1)} fusion(bf16[256,6144]{1,0:T(8,128)(2,1)} %all-gather.5.cloned.1.call-done, bf16[6144,384]{1,0:T(8,128)(2,1)} %param.16), kind=kOutput, calls=%fused_computation.27 | convolution fusion | flops 1208057856 | bytes 8060928 | tf_op jit(solution)/shard_map/dot_general | solution.py:91
  70.5 5.5 %all-gather.3.cloned.1.call-done = bf16[256,6144]{1,0:T(8,128)(2,1)} async-done(((bf16[256,768]{1,0:T(8,128)(2,1)}), bf16[256,6144]{1,0:T(8,128)(2,1)}) %all-gather.3.cloned.1.call-update) | async-done | bytes 3145744 | tf_op jit(solution)/shard_map/all_gather | solution.py:74
  76.0 2.5 convert_reduce_fusion
  78.6 0.3 copy-done
  78.9 1.0 fusion.4
  79.8 7.3 %fusion.5 = f32[256,3,3,128]{0,3,2,1:T(8,128)S(1)} fusion(bf16[3,3,128,6144]{3,2,1,0:T(8,128)(2,1)} %bitcast.122, f32[6144]{0:T(1024)S(1)} %copy-done.5, bf16[256,6144]{1,0:T(8,128)(2,1)S(1)} %copy-done, f32[256]{0:T(256)S(1)} %add_rsqrt_fusion, f32[256]{0:T(256)S(1)} %broadcast_multiply_fusion.4), kind=kOutput, calls=%fused_computation.17 | convolution fusion | flops 3631742976 | bytes 18507776 | tf_op jit(solution)/shard_map/dot_general | solution.py:83
  87.4 0.5 select_reduce_fusion
  87.9 0.3 fusion.16
  88.2 0.4 multiply_reduce_fusion.1
  88.6 0.4 multiply_reduce_fusion.3
  89.0 0.4 fusion.28
  89.8 0.9 add_convert_fusion
  90.6 11.2 %fusion = bf16[256,6144]{1,0:T(8,128)(2,1)} fusion(bf16[256,3,384]{0,2,1:T(8,128)(2,1)} %bitcast.124, bf16[6144,3,384]{2,0,1:T(8,128)(2,1)} %param.14), kind=kOutput, calls=%fused_computation.8 | convolution fusion | flops 3625451520 | bytes 17891328 | tf_op jit(solution)/shard_map/dot_general | solution.py:41
  101.8 0.3 reduce-scatter.6.cloned.1.call-start
  102.1 1.5 convolution_convert_fusion.6
  103.6 5.9 %convolution_convert_fusion.2 = bf16[256,6144]{1,0:T(8,128)(2,1)} fusion(bf16[256,384]{0,1:T(8,128)(2,1)S(1)} %bitcast.129, bf16[6144,384]{1,0:T(8,128)(2,1)} %param.16), kind=kOutput, calls=%fused_computation.10 | convolution fusion | flops 1209532416 | bytes 8060928 | tf_op jit(solution)/shard_map/dot_general | solution.py:41
  109.6 5.5 %fusion.1 = bf16[6144,384]{0,1:T(8,128)(2,1)} fusion(bf16[256,384]{0,1:T(8,128)(2,1)S(1)} %bitcast.130, bf16[256,6144]{1,0:T(8,128)(2,1)} %all-gather.5.cloned.1.call-done), kind=kOutput, calls=%fused_computation.9 | convolution fusion | flops 1210318848 | bytes 8060928 | tf_op jit(solution)/shard_map/dot_general | solution.py:35
  115.1 6.7 %copy.61 = bf16[6144,384]{1,0:T(8,128)(2,1)} copy(bf16[6144,384]{0,1:T(8,128)(2,1)} %fusion.1) | data formatting | bytes 9437184
  121.9 8.9 %convolution_convert_fusion = bf16[6144,1152]{1,0:T(8,128)(2,1)} fusion(bf16[256,1152]{0,1:T(8,128)(2,1)} %bitcast.125, f32[6144]{0:T(1024)S(1)} %copy-done.5, bf16[256,6144]{1,0:T(8,128)(2,1)S(1)} %copy-done, f32[256]{0:T(256)S(1)} %add_rsqrt_fusion, f32[256]{0:T(256)S(1)} %broadcast_multiply_fusion.4), kind=kOutput, calls=%fused_computation.3 | convolution fusion | flops 3638820864 | bytes 17917952 | tf_op jit(solution)/shard_map/dot_general | solution.py:35
  130.9 38.0 %all-reduce.5.cloned.1.call-done = bf16[256,6144]{1,0:T(8,128)(2,1)} async-done(((bf16[256,6144]{1,0:T(8,128)(2,1)}), bf16[256,6144]{1,0:T(8,128)(2,1)}) %all-reduce.5.cloned.1.call-update) | async-done | bytes 3145744 | tf_op jit(solution)/shard_map/psum | solution.py:96
  168.9 4.1 %fusion.7 = (f32[256]{0:T(256)S(1)}, f32[256]{0:T(256)S(1)}, f32[256,6144]{1,0:T(8,128)S(1)}, f32[256,6144]{1,0:T(8,128)S(1)}) fusion(f32[6144]{0:T(1024)} %param.13, bf16[256,6144]{1,0:T(8,128)(2,1)} %all-reduce.5.cloned.1.call-done, f32[256]{0:T(256)S(1)} %add_rsqrt_fusion, f32[256]{0:T(256)S(1)} %broadcast_multiply_fusion.4, bf16[256,6144]{1,0:T(8,128)(2,1)S(1)} %copy-done), kind=kLoop, calls=%fused_computation.19 | loop fusion | flops 12582400 | bytes 18903040 | tf_op jit(solution)/shard_map/reduce_sum | solution.py:100
  173.1 1.0 fusion.20
  174.1 31.3 %reduce-scatter.6.cloned.1.call-done = bf16[256,768]{1,0:T(8,128)(2,1)} async-done(((bf16[256,6144]{1,0:T(8,128)(2,1)}), bf16[256,768]{1,0:T(8,128)(2,1)}) %reduce-scatter.6.cloned.1.call-update) | async-done | bytes 393232 | tf_op jit(solution)/shard_map/reduce_scatter | solution.py:87
  205.4 1.8 add_convert_fusion.1
  207.2 79.7 %reduce-scatter.10.cloned.1.call-done = bf16[384,384]{1,0:T(8,128)(2,1)} async-done(((bf16[6144,384]{1,0:T(8,128)(2,1)}), bf16[384,384]{1,0:T(8,128)(2,1)}) %reduce-scatter.10.cloned.1.call-update) | async-done | bytes 294928
  287.0 1.2 copy.62
  288.2 0.9 copy.51
  289.1 101.7 %reduce-scatter.8.cloned.1.call-done = bf16[384,1152]{1,0:T(8,128)(2,1)} async-done(((bf16[6144,1152]{1,0:T(8,128)(2,1)}), bf16[384,1152]{1,0:T(8,128)(2,1)}) %reduce-scatter.8.cloned.1.call-update) | async-done | bytes 884752 | tf_op jit(solution)/shard_map/reduce_scatter | solution.py:106
  390.8 1.3 multiply_convert_fusion.1
  392.1 0.9 copy.49
  393.0 2.2 copy.50
  (51 shorter events, 1.5 us)
Async XLA Ops:
  7.2 57.9 %all-gather.5.cloned.1.call-start = ((), (), s32[]{:S(2)}) async-start(), calls=%async_computation.7 | async-start | bytes 3538944 | tf_op jit(solution)/shard_map/all_gather | solution.py:75
  13.1 13.9 %all-to-all-start = ((s32[16,1,32]{2,1,0:T(1,128)}), s32[16,1,32]{2,1,0:T(1,128)S(1)}, u32[]{:S(2)}, u32[]{:S(2)}) async-start(s32[16,1,32]{2,1,0:T(1,128)} %all_to_all.9), calls=%async_computation | async-start | bytes 16384 | tf_op jit(solution)/shard_map/all_to_all | solution.py:64
  27.0 15.6 %all-to-all-start.1 = ((bf16[16,32,768]{2,1,0:T(8,128)(2,1)}), bf16[16,32,768]{2,1,0:T(8,128)(2,1)S(1)}, u32[]{:S(2)}, u32[]{:S(2)}) async-start(bf16[16,32,768]{2,1,0:T(8,128)(2,1)} %bitcast.3), calls=%async_computation.1 | async-start | bytes 1572864 | tf_op jit(solution)/shard_map/all_to_all | solution.py:57
  30.6 45.4 %all-gather.3.cloned.1.call-start = ((), (), s32[]{:S(2)}) async-start(), calls=%async_computation.5 | async-start | bytes 3538944 | tf_op jit(solution)/shard_map/all_gather | solution.py:74
  45.9 19.0 %copy-start.7 = (f32[2,128]{1,0:T(2,128)S(1)}, f32[2,128]{1,0:T(2,128)}, u32[]{:S(2)}) copy-start(f32[2,128]{1,0:T(2,128)} %param.15) | copy-start | bytes 3076
  45.9 19.0 %copy-start.6 = (s32[256]{0:T(256)S(1)}, s32[256]{0:T(256)}, u32[]{:S(2)}) copy-start(s32[256]{0:T(256)} %param.12) | copy-start | bytes 3076
  45.9 123.0 %all-reduce.5.cloned.1.call-start = ((), (), s32[]{:S(2)}) async-start(), calls=%async_computation.8 | async-start | bytes 6291456 | tf_op jit(solution)/shard_map/psum | solution.py:96
  70.3 9.5 %copy-start.5 = (f32[6144]{0:T(1024)S(1)}, f32[6144]{0:T(1024)}, u32[]{:S(2)}) copy-start(f32[6144]{0:T(1024)} %param.13) | copy-start | bytes 73732
  76.0 2.8 copy-start
  87.2 2.5 copy-start.1
  87.9 1.1 copy-start.4
  101.8 103.6 %reduce-scatter.6.cloned.1.call-start = ((), (), s32[]{:S(2)}) async-start(), calls=%async_computation.6 | async-start | bytes 3538944 | tf_op jit(solution)/shard_map/reduce_scatter | solution.py:87
  109.6 177.4 %reduce-scatter.10.cloned.1.call-start = ((), (), s32[]{:S(2)}) async-start(), calls=%async_computation.10 | async-start | bytes 5013504
  121.9 268.9 %reduce-scatter.8.cloned.1.call-start = ((), (), s32[]{:S(2)}) async-start(), calls=%async_computation.9 | async-start | bytes 15040512 | tf_op jit(solution)/shard_map/reduce_scatter | solution.py:106
  130.9 74.5 %copy-start.2 = (bf16[256,768]{1,0:T(8,128)(2,1)S(1)}, bf16[256,768]{1,0:T(8,128)(2,1)}, u32[]{:S(2)}) copy-start(bf16[256,768]{1,0:T(8,128)(2,1)} %scatter_custom_fusion.2) | copy-start | bytes 1179652
  168.9 4.2 %copy-start.3 = (bf16[256,768]{1,0:T(8,128)(2,1)S(1)}, bf16[256,768]{1,0:T(8,128)(2,1)}, u32[]{:S(2)}) copy-start(bf16[256,768]{1,0:T(8,128)(2,1)} %param.17) | copy-start | bytes 1179652
Sparse Core Ops, SparseCore 0:
  9.7 31.5 all-gather.4
  46.0 29.9 all-gather.2
  102.0 66.9 all-reduce.4
  171.2 34.1 reduce-scatter.5
  208.6 78.3 reduce-scatter.9
  290.3 100.3 reduce-scatter.7
where the time goes:
time: 403 us; the launch traced here: 402 us
  waiting for transfers between devices  271 us (67%)
  matrix products  47.5 us (12%)
  local copies, waits for them, and re-layouts  40.4 us (10%)
  other arithmetic  16.8 us (4%)
  between operations  14.4 us (4%)
  starting transfers between devices  11.8 us (3%)
    reduce_scatter x1, waiting for transfers between devices, shards(): lax.psum_scatter(contract_rows(normed, d_proj_bf).astype(jnp.bfloat16), '...  102 us
    unnamed x7, waiting for transfers between devices  80.5 us
    psum x1, waiting for transfers between devices, shards(): d_normed = lax.psum(d_part.astype(jnp.bfloat16), 'mp').astype(jnp.float32)  38 us
    reduce_scatter x1, waiting for transfers between devices, shards(): lax.psum_scatter(contract_cols(heads_out, w_out).astype(jnp.bfloat16), 'm...  31.3 us
    unnamed x21, local copies, waits for them, and re-layouts  30 us
    dot_general x2, matrix products, contract_cols(): lax.dot_general(left, right, (((1,), (1,)), ((), ())), preferred_element_...  17.1 us
    dot_general x2, matrix products, contract_rows(): lax.dot_general(left, right, (((0,), (0,)), ((), ())), preferred_element_...  14.4 us
    all_to_all x1, waiting for transfers between devices, shards(): lax.all_to_all(outbox.reshape(groups, slot_size, part_width), 'dp', split...  10.6 us
  transfers between devices with their start and end apart: 8, of which 7 were waited for; matrix products, arithmetic and copies ran while one was open for 18% of the time, Pallas kernels for 0%

commit v1 on v0

--- a/solution.py
+++ b/solution.py
@@ -1,11 +1,274 @@
+import functools
 import math
 
 import jax
 import jax.numpy as jnp
 from jax import lax
+from jax.experimental import pallas as pl
+from jax.experimental.pallas import tpu as pltpu
 from jax.sharding import PartitionSpec as P
 
 DH = 128
+MESH = pl.DeviceIdType.MESH
+F32 = jnp.float32
+BF16 = jnp.bfloat16
+
+
+class Place:
+    def __init__(self):
+        self.g, self.m = lax.axis_index("dp"), lax.axis_index("mp")
+        self.x, self.y = self.g // 4, self.g % 4
+        self.z, self.c = self.m // 2, self.m % 2
+        c = self.c
+        self.a = self.x * (1 - c) + self.y * c
+        self.b = self.x * c + self.y * (1 - c)
+
+    def along_a(self, k):
+        x, y = (self.x + k * (1 - self.c)) % 4, (self.y + k * self.c) % 4
+        return (x * 4 + y, self.m)
+
+    def along_b(self, k):
+        x, y = (self.x + k * self.c) % 4, (self.y + k * (1 - self.c)) % 4
+        return (x * 4 + y, self.m)
+
+    def along_z(self, k):
+        return (self.g, ((self.z + k) % 4) * 2 + self.c)
+
+    def along_m(self, k):
+        return (self.g, (self.m + k) % 8)
+
+    def sibling(self):
+        return (self.g, self.z * 2 + 1 - self.c)
+
+    def block(self, q, j):
+        c = self.c
+        return 4 * (q * (1 - c) + j * c) + q * c + j * (1 - c)
+
+
+def remote(src, dst, send, recv, device):
+    return pltpu.make_async_remote_copy(
+        src_ref=src, dst_ref=dst, send_sem=send, recv_sem=recv, device_id=device, device_id_type=MESH
+    )
+
+
+def greet(devices):
+    barrier = pltpu.get_barrier_semaphore()
+    for device in devices:
+        pl.semaphore_signal(barrier, inc=1, device_id=device, device_id_type=MESH)
+    pl.semaphore_wait(barrier, len(devices))
+
+
+def nt_dot(left, right):
+    return lax.dot_general(left, right, (((1,), (1,)), ((), ())), preferred_element_type=F32)
+
+
+def tn_dot(left, right):
+    return lax.dot_general(left, right, (((0,), (0,)), ((), ())), preferred_element_type=F32)
+
+
+def second(
+    scale,
+    normed, cot, heads, dproj, w_qkv, w_out, packed, cot_part, mean, rstd, gain,
+    output, input_grad, qkv_grad, out_grad,
+    cot_a, normed_a, heads_a, dproj_a, wq, wo,
+    sib_out, sib_in, z_out, z_in, dn_sib_out, dn_sib_in, dn_z_out, dn_z_in,
+    og_out, og_in, qg_out, qg_in, st_out, st_in, st_pad, own_og, own_qg, own_at, own_dn,
+    wsem, lsem, cs, cr, ns, nr, hs, hr, ps, pr, ss, sr, zs, zr, dss, dsr, dzs, dzr, os_, or_, qs, qr, ts, tr,
+):
+    at = Place()
+    a, b, c, z, m = at.a, at.b, at.c, at.z, at.m
+    width = 768
+    half = 384
+    load_wo = pltpu.make_async_copy(w_out, wo, wsem.at[0])
+    load_wq = pltpu.make_async_copy(w_qkv, wq, wsem.at[1])
+    load_wo.start()
+    load_wq.start()
+    greet([at.along_a(k) for k in (1, 2, 3)] + [at.along_b(k) for k in (1, 2, 3)] + [at.along_m(k) for k in range(1, 8)])
+
+    mine = pl.ds(pl.multiple_of(a * 256, 256), 256)
+
+    def spread(full, buf, send, recv):
+        copies = []
+        for k in (1, 2, 3):
+            q = (a + k) % 4
+            for j in range(4):
+                cols = pl.ds(pl.multiple_of(at.block(q, j) * half, half), half)
+                copies.append(
+                    remote(
+                        full.at[:, cols], buf.at[mine, pl.ds(j * half, half)],
+                        send.at[k - 1, j], recv.at[k - 1, j], at.along_a(k),
+                    )
+                )
+        return copies
+
+    def keep(full, buf, sem):
+        copies = []
+        for j in range(4):
+            cols = pl.ds(pl.multiple_of(at.block(a, j) * half, half), half)
+            copies.append(pltpu.make_async_copy(full.at[:, cols], buf.at[mine, pl.ds(j * half, half)], sem.at[j]))
+        return copies
+
+    def gather(part, buf, send, recv):
+        return [remote(part, buf.at[mine, :], send.at[k - 1], recv.at[k - 1], at.along_a(k)) for k in (1, 2, 3)]
+
+    heads_copies = gather(heads, heads_a, hs, hr)
+    cot_copies = spread(cot, cot_a, cs, cr)
+    dproj_copies = gather(dproj, dproj_a, ps, pr)
+    normed_copies = spread(normed, normed_a, ns, nr)
+    local = keep(cot, cot_a, lsem.at[0]) + keep(normed, normed_a, lsem.at[1])
+    for copy in heads_copies + cot_copies + dproj_copies + normed_copies + local:
+        copy.start()
+    heads_a[mine, :] = heads[...]
+    dproj_a[mine, :] = dproj[...]
+
+    def attn_term(shard):
+        rows = pl.ds(pl.multiple_of(shard * width, width), width)
+        return nt_dot(heads[...], wo[rows, :])
+
+    def dn_term(shard):
+        rows = pl.ds(pl.multiple_of(shard * width, width), width)
+        total = nt_dot(dproj[:, 0:half], wq[0, rows, :])
+        total += nt_dot(dproj[:, half : 2 * half], wq[1, rows, :])
+        return total + nt_dot(dproj[:, 2 * half : 3 * half], wq[2, rows, :])
+
+    def to_sibling(term, out, into, send, recv):
+        def step(k, carry):
+            out[k] = term(((z + 1 + k) % 4) * 2 + 1 - c).astype(BF16)
+            remote(out.at[k], into.at[k], send.at[k], recv.at[k], at.sibling()).start()
+            return carry
+
+        lax.fori_loop(0, 4, step, 0)
+
+    def along_z(term, sib_o, sib, sib_send, sib_recv, out, into, send, recv, own):
+        def step(k, carry):
+            value = term(((z + 1 + k) % 4) * 2 + c)
+            remote(sib_o.at[k], sib.at[k], sib_send.at[k], sib_recv.at[k], at.sibling()).wait()
+            out[k] = (value + sib[k].astype(F32)).astype(BF16)
+            remote(out.at[k], into.at[k], send.at[k], recv.at[k], at.along_z(1 + k)).start()
+            return carry
+
+        lax.fori_loop(0, 3, step, 0)
+        value = term(z * 2 + c)
+        remote(sib_o.at[3], sib.at[3], sib_send.at[3], sib_recv.at[3], at.sibling()).wait()
+        own[...] = value + sib[3].astype(F32)
+
+    load_wo.wait()
+    to_sibling(attn_term, sib_out, sib_in, ss, sr)
+    load_wq.wait()
+    to_sibling(dn_term, dn_sib_out, dn_sib_in, dss, dsr)
+    along_z(attn_term, sib_out, sib_in, ss, sr, z_out, z_in, zs, zr, own_at)
+    along_z(dn_term, dn_sib_out, dn_sib_in, dss, dsr, dn_z_out, dn_z_in, dzs, dzr, own_dn)
+
+    for copy in local:
+        copy.wait()
+    for copy in heads_copies + cot_copies:
+        copy.wait()
+
+    def out_term(j):
+        return tn_dot(cot_a[:, pl.ds(pl.multiple_of(j * half, half), half)], heads_a[...])
+
+    def out_step(k, carry):
+        og_out[k] = out_term((b + 1 + k) % 4).astype(BF16)
+        remote(og_out.at[k], og_in.at[k], os_.at[k], or_.at[k], at.along_b(1 + k)).start()
+        return carry
+
+    lax.fori_loop(0, 3, out_step, 0)
+    own_og[...] = out_term(b)
+
+    for copy in dproj_copies + normed_copies:
+        copy.wait()
+
+    def qkv_term(j):
+        return tn_dot(normed_a[:, pl.ds(pl.multiple_of(j * half, half), half)], dproj_a[...])
+
+    def qkv_step(k, carry):
+        qg_out[k] = qkv_term((b + 1 + k) % 4).astype(BF16)
+        remote(qg_out.at[k], qg_in.at[k], qs.at[k], qr.at[k], at.along_b(1 + k)).start()
+        return carry
+
+    lax.fori_loop(0, 3, qkv_step, 0)
+    own_qg[...] = qkv_term(b)
+
+    total = own_at[...]
+    for k in range(3):
+        remote(z_out.at[k], z_in.at[k], zs.at[k], zr.at[k], at.along_z(1 + k)).wait()
+        total += z_in[k].astype(F32)
+    output[...] = (packed[...].astype(F32) + total).astype(BF16)
+
+    total = own_dn[...]
+    for k in range(3):
+        remote(dn_z_out.at[k], dn_z_in.at[k], dzs.at[k], dzr.at[k], at.along_z(1 + k)).wait()
+        total += dn_z_in[k].astype(F32)
+    u = total * gain[pl.ds(m, 1), :]
+    unit = (packed[...].astype(F32) - mean[...]) * rstd[...]
+    sum_u = jnp.sum(u, -1, keepdims=True)
+    sum_uu = jnp.sum(u * unit, -1, keepdims=True)
+    own_dn[...] = u
+    lane = lax.broadcasted_iota(jnp.int32, (256, 128), 1)
+    pair = jnp.where(lane == 0, sum_u, jnp.where(lane == 1, sum_uu, 0.0))
+    st_out[...] = pair.T[0:8]
+    stats = [remote(st_out, st_in.at[k - 1], ts.at[k - 1], tr.at[k - 1], at.along_m(k)) for k in range(1, 8)]
+    for copy in stats:
+        copy.start()
+    sums = st_out[...]
+    for k in range(7):
+        stats[k].wait()
+        sums += st_in[k]
+    st_pad[...] = jnp.zeros_like(st_pad)
+    st_pad[0:8, :] = sums * (1.0 / 6144.0)
+    means = st_pad[...].T
+    grad = rstd[...] * (own_dn[...] - means[:, 0:1] - unit * means[:, 1:2])
+    input_grad[...] = (cot_part[...].astype(F32) + grad).astype(BF16)
+
+    total = own_og[...]
+    for k in range(3):
+        remote(og_out.at[k], og_in.at[k], os_.at[k], or_.at[k], at.along_b(1 + k)).wait()
+        total += og_in[k].astype(F32)
+    out_grad[...] = (total * scale).astype(BF16)
+
+    for k in range(3):
+        remote(qg_out.at[k], qg_in.at[k], qs.at[k], qr.at[k], at.along_b(1 + k)).wait()
+    for t in range(3):
+        cols = slice(t * half, (t + 1) * half)
+        total = own_qg[:, cols]
+        for k in range(3):
+            total += qg_in[k, :, cols].astype(F32)
+        qkv_grad[t] = (total * scale).astype(BF16)
+
+
+def call_second(normed, cot, heads, dproj, w_qkv, w_out, packed, cot_part, mean, rstd, gain, scale):
+    vmem = pl.BlockSpec(memory_space=pltpu.VMEM)
+    anywhere = pl.BlockSpec(memory_space=pl.ANY)
+    dma = pltpu.SemaphoreType.DMA
+    V = pltpu.VMEM
+    return pl.pallas_call(
+        functools.partial(second, scale),
+        out_shape=(
+            jax.ShapeDtypeStruct((256, 768), BF16),
+            jax.ShapeDtypeStruct((256, 768), BF16),
+            jax.ShapeDtypeStruct((3, 384, 384), BF16),
+            jax.ShapeDtypeStruct((384, 384), BF16),
+        ),
+        in_specs=[anywhere, anywhere, vmem, vmem, anywhere, anywhere, vmem, vmem, vmem, vmem, vmem],
+        out_specs=(vmem,) * 4,
+        scratch_shapes=[
+            V((1024, 1536), BF16), V((1024, 1536), BF16), V((1024, 384), BF16), V((1024, 1152), BF16),
+            V((3, 6144, 384), BF16), V((6144, 384), BF16),
+            V((4, 256, 768), BF16), V((4, 256, 768), BF16), V((3, 256, 768), BF16), V((3, 256, 768), BF16),
+            V((4, 256, 768), BF16), V((4, 256, 768), BF16), V((3, 256, 768), BF16), V((3, 256, 768), BF16),
+            V((3, 384, 384), BF16), V((3, 384, 384), BF16), V((3, 384, 1152), BF16), V((3, 384, 1152), BF16),
+            V((8, 256), F32), V((7, 8, 256), F32), V((128, 256), F32),
+            V((384, 384), F32), V((384, 1152), F32), V((256, 768), F32), V((256, 768), F32),
+            dma((2,)), dma((2, 4)), dma((3, 4)), dma((3, 4)), dma((3, 4)), dma((3, 4)),
+            dma((3,)), dma((3,)), dma((3,)), dma((3,)),
+            dma((4,)), dma((4,)), dma((3,)), dma((3,)), dma((4,)), dma((4,)), dma((3,)), dma((3,)),
+            dma((3,)), dma((3,)), dma((3,)), dma((3,)), dma((7,)), dma((7,)),
+        ],
+        compiler_params=pltpu.CompilerParams(
+            collective_id=1, has_side_effects=True, vmem_limit_bytes=62 << 20
+        ),
+        name="second",
+    )(normed, cot, heads, dproj, w_qkv, w_out, packed, cot_part, mean, rstd, gain)
 
 
 def norm_heads(values, gain):
@@ -75,7 +338,8 @@
         lax.all_gather(cotangent, "mp", axis=1, tiled=True),
     )
     wide = whole_rows.astype(jnp.float32)
-    center = wide - jnp.mean(wide, -1, keepdims=True)
+    mean = jnp.mean(wide, -1, keepdims=True)
+    center = wide - mean
     rstd = lax.rsqrt(jnp.mean(center * center, -1, keepdims=True) + 1e-06)
     unit_rows = center * rstd
     normed = (unit_rows * ln_gain).astype(jnp.bfloat16)
@@ -84,42 +348,15 @@
         group_rows, 3, local_width
     )
     heads_out, backward = jax.vjp(lambda values: attend(values, segment, qk_gain), projected)
-    attn = lax.psum_scatter(
-        contract_cols(heads_out, w_out).astype(jnp.bfloat16), "mp", scatter_dimension=1, tiled=True
-    ).astype(jnp.float32)
-    output = (packed.astype(jnp.float32) + attn).astype(jnp.bfloat16)
     d_heads = jnp.dot(whole_cot, w_out, preferred_element_type=jnp.float32).astype(jnp.bfloat16)
     (d_projected,) = backward(d_heads)
     d_proj_bf = d_projected.astype(jnp.bfloat16).reshape(group_rows, 3 * local_width)
-    d_part = contract_cols(d_proj_bf, w_flat)
-    my_index = lax.axis_index("mp")
-    d_normed = lax.psum(d_part.astype(jnp.bfloat16), "mp").astype(jnp.float32)
-    d_unit = d_normed * ln_gain
-    d_full = rstd * (
-        d_unit
-        - jnp.mean(d_unit, -1, keepdims=True)
-        - unit_rows * jnp.mean(d_unit * unit_rows, -1, keepdims=True)
-    )
-    d_input = lax.dynamic_slice_in_dim(d_full, my_index * part_width, part_width, 1)
-    input_grad = (cotangent.astype(jnp.float32) + d_input).astype(jnp.bfloat16)
-    sum_qkv, sum_out = (
-        lax.psum_scatter(
-            contract_rows(normed, d_proj_bf).astype(jnp.bfloat16),
-            "dp",
-            scatter_dimension=0,
-            tiled=True,
-        ).astype(jnp.float32),
-        lax.psum_scatter(
-            contract_rows(whole_cot, heads_out).astype(jnp.bfloat16),
-            "dp",
-            scatter_dimension=0,
-            tiled=True,
-        ).astype(jnp.float32),
-    )
     scale_grad = 1.0 / math.sqrt(group_rows * groups)
-    qkv_grad = (sum_qkv * scale_grad).reshape(-1, 3, local_width).astype(jnp.bfloat16)
-    out_grad = (sum_out * scale_grad).astype(jnp.bfloat16)
-    return (output, input_grad, qkv_grad, out_grad)
+    output, input_grad, qkv_grad, out_grad = call_second(
+        normed, whole_cot, heads_out, d_proj_bf, jnp.transpose(w_qkv, (1, 0, 2)), w_out,
+        packed, cotangent, mean, rstd, ln_gain.reshape(8, 768), scale_grad,
+    )
+    return (output, input_grad, jnp.transpose(qkv_grad, (1, 0, 2)), out_grad)
 
 
 def solution(mesh):

time: 403 us -> 201 us (0.50)
  waiting for transfers between devices: 271 us -> 19.8 us
  Pallas kernels: 0 us -> 90.4 us
  matrix products: 47.5 us -> 15.7 us
  other arithmetic: 16.8 us -> 9.05 us
    reduce_scatter x2 -> x0, waiting for transfers between devices: 133 us -> none  [the longest x1 102 us: shards(): lax.psum_scatter(contract_rows(normed, d_proj_bf).astype(jnp.bfloat16), '...]
    pallas_call x0 -> x1, Pallas kernels: none -> 90.4 us  [call_second(): pl.pallas_call(functools.partial(second, scale), out_shape=(jax.ShapeDtyp...]
    unnamed x7 -> x2, waiting for transfers between devices: 80.5 us -> 0.7 us
    psum x1 -> x0, waiting for transfers between devices: 38 us -> none  [shards(): d_normed = lax.psum(d_part.astype(jnp.bfloat16), 'mp').astype(jnp.float32)]
    dot_general x4 -> x0, matrix products: 31.5 us -> none  [the longest x2 17.1 us: contract_cols(): lax.dot_general(left, right, (((1,), (1,)), ((), ())), preferred_element_...]
    unnamed x21 -> x17, local copies, waits for them, and re-layouts: 30 us -> 25.5 us
    reduce_sum x2 -> x1, other arithmetic: 6.68 us -> 2.54 us  [shards(): mean = jnp.mean(wide, -1, keepdims=True)]
  transfers between devices with their start and end apart: 8 -> 4, of which waited for: 7 -> 3; matrix products, arithmetic and copies ran while one was open for 18% -> 19% of each run, Pallas kernels for 0% -> 0%
where the time goes in v1:
time: 201 us; the launch traced here: 200 us
  Pallas kernels  90.4 us (45%)
  local copies, waits for them, and re-layouts  39.1 us (19%)
  waiting for transfers between devices  19.8 us (10%)
  matrix products  15.7 us (8%)
  between operations  14.3 us (7%)
  starting transfers between devices  11.3 us (6%)
  other arithmetic  9.05 us (5%)
    pallas_call x1, Pallas kernels, call_second(): pl.pallas_call(functools.partial(second, scale), out_shape=(jax.ShapeDtyp...  90.4 us
    unnamed x17, local copies, waits for them, and re-layouts  25.5 us
    all_to_all x1, waiting for transfers between devices, shards(): lax.all_to_all(outbox.reshape(groups, slot_size, part_width), 'dp', split...  10.6 us
    dot_general x1, matrix products, shards(): jnp.dot(normed, w_flat, preferred_element_type=jnp.float32)  8.24 us
    all_to_all x1, starting transfers between devices, shards(): lax.all_to_all(address.reshape(groups, slot_size), 'dp', split_axis=0, co...  7.58 us
    dot_general x1, matrix products, shards(): jnp.dot(whole_cot, w_out, preferred_element_type=jnp.float32)  5.23 us
    all_gather x1, waiting for transfers between devices, shards(): lax.all_gather(packed, 'mp', axis=1, tiled=True)  5.16 us
  transfers between devices with their start and end apart: 4, of which 3 were waited for; matrix products, arithmetic and copies ran while one was open for 19% of the time, Pallas kernels for 0%

profile of v1, /device:TPU:1, one launch (start us, length us, event | category | flops | bytes accessed | tf_op | source)
XLA Modules:
  0.0 199.6 jit_solution(14494689801508544028)
XLA Ops:
  7.2 0.7 all-gather.5.cloned.1.call-update
  7.9 0.7 fusion.27
  8.6 0.6 reduce-window.6
  9.2 0.2 slice_reduce_fusion.2
  9.4 0.8 fusion.26
  10.2 0.7 compare_select_fusion.1
  10.8 1.6 scatter_custom_fusion
  12.4 0.7 all_to_all.9
  13.1 7.6 %all-to-all-start = ((s32[16,1,32]{2,1,0:T(1,128)}), s32[16,1,32]{2,1,0:T(1,128)S(1)}, u32[]{:S(2)}, u32[]{:S(2)}) async-start(s32[16,1,32]{2,1,0:T(1,128)} %all_to_all.9), calls=%async_computation | async-start | bytes 16384 | tf_op jit(solution)/shard_map/all_to_all | solution.py:327
  20.7 3.1 %scatter_custom_fusion.1 = bf16[512,768]{1,0:T(8,128)(2,1)} fusion(s32[256]{0:T(256)S(1)} %compare_select_fusion.1, bf16[256,768]{1,0:T(8,128)(2,1)} %param.9, bf16[]{:T(256)} %constant.16.clone.1), kind=kCustom, calls=%fused_computation.46 | custom fusion | bytes 786944 | tf_op jit(solution)/shard_map/scatter | solution.py:317
  23.7 3.3 %all-to-all-done = s32[16,1,32]{2,1,0:T(1,128)S(1)} async-done(((s32[16,1,32]{2,1,0:T(1,128)}), s32[16,1,32]{2,1,0:T(1,128)S(1)}, u32[]{:S(2)}, u32[]{:S(2)}) %all-to-all-start) | async-done | bytes 2080 | tf_op jit(solution)/shard_map/all_to_all | solution.py:327
  27.0 3.6 %all-to-all-start.1 = ((bf16[16,32,768]{2,1,0:T(8,128)(2,1)}), bf16[16,32,768]{2,1,0:T(8,128)(2,1)S(1)}, u32[]{:S(2)}, u32[]{:S(2)}) async-start(bf16[16,32,768]{2,1,0:T(8,128)(2,1)} %bitcast.3), calls=%async_computation.1 | async-start | bytes 1572864 | tf_op jit(solution)/shard_map/all_to_all | solution.py:320
  30.7 0.5 broadcast.246
  31.2 0.7 reduce.7
  31.9 0.1 reshape.206
  32.0 10.6 %all-to-all-done.1 = bf16[16,32,768]{2,1,0:T(8,128)(2,1)S(1)} async-done(((bf16[16,32,768]{2,1,0:T(8,128)(2,1)}), bf16[16,32,768]{2,1,0:T(8,128)(2,1)S(1)}, u32[]{:S(2)}, u32[]{:S(2)}) %all-to-all-start.1) | async-done | bytes 786464 | tf_op jit(solution)/shard_map/all_to_all | solution.py:320
  42.6 3.3 %scatter_custom_fusion.2.packed = bf16[256,768]{1,0:T(8,128)(2,1)} fusion(s32[512]{0:T(512)S(1)} %bitcast.118, bf16[512,768]{1,0:T(8,128)(2,1)S(1)} %bitcast.113, bf16[]{:T(256)} %constant.16.clone.1), kind=kCustom, calls=%fused_computation.51 | custom fusion | bytes 393218 | tf_op jit(solution)/shard_map/scatter | solution.py:334
  46.0 18.8 %copy.24 = bf16[6144,3,384]{0,2,1:T(8,128)(2,1)} copy(bf16[6144,3,384]{2,0,1:T(8,128)(2,1)} %param.14) | data formatting | bytes 28311552 | tf_op args[5]
  64.7 0.6 reshape.211.gain
  65.3 0.1 broadcast_compare_fusion
  65.5 5.2 %convolution_convert_fusion.2 = bf16[256,384]{1,0:T(8,128)(2,1)S(1)} fusion(bf16[256,6144]{1,0:T(8,128)(2,1)} %all-gather.5.cloned.1.call-done.cot, bf16[6144,384]{1,0:T(8,128)(2,1)} %w_out.1), kind=kOutput, calls=%fused_computation.18 | convolution fusion | flops 1208057856 | bytes 8060928 | tf_op jit(solution)/shard_map/dot_general | solution.py:351
  70.7 0.1 copy.28
  70.9 5.2 %all-gather.3.cloned.1.call-done = bf16[256,6144]{1,0:T(8,128)(2,1)} async-done(((bf16[256,768]{1,0:T(8,128)(2,1)}), bf16[256,6144]{1,0:T(8,128)(2,1)}) %all-gather.3.cloned.1.call-update) | async-done | bytes 3145744 | tf_op jit(solution)/shard_map/all_gather | solution.py:337
  76.0 2.5 %convert_reduce_fusion = f32[256]{0:T(256)S(1)} fusion(bf16[256,6144]{1,0:T(8,128)(2,1)} %all-gather.3.cloned.1.call-done), kind=kLoop, calls=%fused_computation.4 | loop fusion | flops 3145472 | bytes 3146752 | tf_op jit(solution)/shard_map/reduce_sum | solution.py:341
  78.6 0.3 copy-done
  78.9 1.0 fusion.2
  79.8 1.4 fusion.4.normed
  81.2 8.2 %fusion.5 = f32[256,3,3,128]{0,3,2,1:T(8,128)S(1)} fusion(bf16[3,3,128,6144]{3,2,1,0:T(8,128)(2,1)} %bitcast.108, bf16[256,6144]{1,0:T(8,128)(2,1)S(1)} %fusion.4.normed), kind=kOutput, calls=%fused_computation.10 | convolution fusion | flops 3623878656 | bytes 18481152 | tf_op jit(solution)/shard_map/dot_general | solution.py:347
  89.5 0.1 slice_reduce_fusion
  89.6 0.1 multiply_reduce_fusion.3
  89.7 0.5 select_reduce_fusion
  90.2 0.3 convolution_convert_fusion.3
  90.4 0.3 fusion.15
  90.8 0.4 multiply_reduce_fusion
  91.1 0.4 multiply_reduce_fusion.2
  91.6 0.4 fusion.23
  92.0 0.2 add_bitcast_fusion.1
  92.3 0.1 add_bitcast_fusion
  92.4 0.1 add_convert_fusion
  92.4 1.1 copy.34.dproj
  93.5 0.8 copy.33.heads
  94.3 0.8 copy.36.rstd
  95.1 0.8 copy.35.mean
  95.9 90.4 %second.1 = (bf16[256,768]{1,0:T(8,128)(2,1)}, bf16[256,768]{1,0:T(8,128)(2,1)}, bf16[3,384,384]{2,1,0:T(8,128)(2,1)}, bf16[384,384]{1,0:T(8,128)(2,1)}) custom-call(bf16[256,6144]{1,0:T(8,128)(2,1)} %copy-done.1, bf16[256,6144]{1,0:T(8,128)(2,1)} %all-gather.5.cloned.1.call-done.cot, bf16[256,384]{1,0:T(8,128)(2,1)} %copy.33.heads, ...), custom_call_target="tpu_custom_call" | custom-call | tf_op jit(solution)/shard_map/second/pallas_call | solution.py:244
  186.3 1.8 copy.51
  188.1 1.8 copy.52
  189.9 2.2 %copy.53 = bf16[384,3,384]{2,0,1:T(8,128)(2,1)} copy(bf16[384,3,384]{2,0,1:T(8,128)(2,1)} %bitcast.110) | data formatting | bytes 1769472
  192.1 0.7 copy.54
  (30 shorter events, 0.3 us)
Async XLA Ops:
  7.2 58.3 %all-gather.5.cloned.1.call-start = ((), (), s32[]{:S(2)}) async-start(), calls=%async_computation.3 | async-start | bytes 3538944 | tf_op jit(solution)/shard_map/all_gather | solution.py:338
  13.1 13.9 %all-to-all-start = ((s32[16,1,32]{2,1,0:T(1,128)}), s32[16,1,32]{2,1,0:T(1,128)S(1)}, u32[]{:S(2)}, u32[]{:S(2)}) async-start(s32[16,1,32]{2,1,0:T(1,128)} %all_to_all.9), calls=%async_computation | async-start | bytes 16384 | tf_op jit(solution)/shard_map/all_to_all | solution.py:327
  27.0 15.6 %all-to-all-start.1 = ((bf16[16,32,768]{2,1,0:T(8,128)(2,1)}), bf16[16,32,768]{2,1,0:T(8,128)(2,1)S(1)}, u32[]{:S(2)}, u32[]{:S(2)}) async-start(bf16[16,32,768]{2,1,0:T(8,128)(2,1)} %bitcast.3), calls=%async_computation.1 | async-start | bytes 1572864 | tf_op jit(solution)/shard_map/all_to_all | solution.py:320
  30.6 45.4 %all-gather.3.cloned.1.call-start = ((), (), s32[]{:S(2)}) async-start(), calls=%async_computation.2 | async-start | bytes 3538944 | tf_op jit(solution)/shard_map/all_gather | solution.py:337
  45.9 18.8 %copy-start.3 = (f32[6144]{0:T(1024)S(1)}, f32[6144]{0:T(1024)}, u32[]{:S(2)}) copy-start(f32[6144]{0:T(1024)} %param.13) | copy-start | bytes 73732
  45.9 19.4 %copy-start.5 = (f32[2,128]{1,0:T(2,128)S(1)}, f32[2,128]{1,0:T(2,128)}, u32[]{:S(2)}) copy-start(f32[2,128]{1,0:T(2,128)} %param.15) | copy-start | bytes 3076
  45.9 19.4 %copy-start.4 = (s32[256]{0:T(256)S(1)}, s32[256]{0:T(256)}, u32[]{:S(2)}) copy-start(s32[256]{0:T(256)} %param.12) | copy-start | bytes 3076
  76.0 2.8 %copy-start = (bf16[256,6144]{1,0:T(8,128)(2,1)S(1)}, bf16[256,6144]{1,0:T(8,128)(2,1)}, u32[]{:S(2)}) copy-start(bf16[256,6144]{1,0:T(8,128)(2,1)} %all-gather.3.cloned.1.call-done) | copy-start | bytes 9437188
  81.2 8.3 %copy-start.1 = (bf16[256,6144]{1,0:T(8,128)(2,1)}, bf16[256,6144]{1,0:T(8,128)(2,1)S(1)}, u32[]{:S(2)}) copy-start(bf16[256,6144]{1,0:T(8,128)(2,1)S(1)} %fusion.4.normed) | copy-start | bytes 9437188
  186.3 5.8 %copy-start.2 = (bf16[384,384]{1,0:T(8,128)(2,1)S(1)}, bf16[384,384]{1,0:T(8,128)(2,1)}, u32[]{:S(2)}) copy-start(bf16[384,384]{1,0:T(8,128)(2,1)} %get-tuple-element.38) | copy-start | bytes 884740
Sparse Core Ops, SparseCore 0:
  9.7 31.5 all-gather.4
  46.0 29.9 all-gather.2

commit v2 on v1

v2 whole, which is shorter than its diff:
```python
import functools
import math

import jax
import jax.numpy as jnp
from jax import lax
from jax.experimental import pallas as pl
from jax.experimental.pallas import tpu as pltpu
from jax.sharding import PartitionSpec as P

DH = 128
MESH = pl.DeviceIdType.MESH
F32 = jnp.float32
BF16 = jnp.bfloat16


class Place:
    def __init__(self):
        self.g, self.m = lax.axis_index("dp"), lax.axis_index("mp")
        self.x, self.y = self.g // 4, self.g % 4
        self.z, self.c = self.m // 2, self.m % 2
        c = self.c
        self.a = self.x * (1 - c) + self.y * c
        self.b = self.x * c + self.y * (1 - c)

    def along_a(self, k):
        x, y = (self.x + k * (1 - self.c)) % 4, (self.y + k * self.c) % 4
        return (x * 4 + y, self.m)

    def along_b(self, k):
        x, y = (self.x + k * self.c) % 4, (self.y + k * (1 - self.c)) % 4
        return (x * 4 + y, self.m)

    def along_z(self, k):
        return (self.g, ((self.z + k) % 4) * 2 + self.c)

    def along_m(self, k):
        return (self.g, (self.m + k) % 8)

    def over_xy(self, dx, dy):
        return (((self.x + dx) % 4) * 4 + (self.y + dy) % 4, self.m)

    def sibling(self):
        return (self.g, self.z * 2 + 1 - self.c)

    def block(self, q, j):
        c = self.c
        return 4 * (q * (1 - c) + j * c) + q * c + j * (1 - c)


def remote(src, dst, send, recv, device):
    return pltpu.make_async_remote_copy(
        src_ref=src, dst_ref=dst, send_sem=send, recv_sem=recv, device_id=device, device_id_type=MESH
    )


def nt_dot(left, right):
    return lax.dot_general(left, right, (((1,), (1,)), ((), ())), preferred_element_type=F32)


def tn_dot(left, right):
    return lax.dot_general(left, right, (((0,), (0,)), ((), ())), preferred_element_type=F32)


def whole(
    scale,
    patches, dest_group, dest_row, segment, gain, w_qkv, qk_gain, w_out, cot,
    output, input_grad, qkv_grad, out_grad,
    outbox, inbox, packed, cot_full, normed_full, cot_a, normed_a, heads_a, dproj_a, wq, wo,
    proj, d_heads, heads, dproj, columns, places, st_pad, st_out, st_in, en_out, en_in,
    sib_in, z_in, dn_sib_out, dn_sib_in, dn_z_out, dn_z_in, og_in, qg_in,
    own_og, own_qg, own_at, own_dn,
    wsem, rs, rr, cz, czr, cb, cbr, nz, nzr, nb, nbr, sts, str_, ens, enr,
    cs, cr, cl, ns, nr, nl, hs, hr, ps, pr, ss, sr, zs, zr, dss, dsr, dzs, dzr, os_, or_, qs, qr,
):
    at = Place()
    a, b, c, z, m, g = at.a, at.b, at.c, at.z, at.m, at.g
    width, half, rows = 768, 384, 256
    load_wo = pltpu.make_async_copy(w_out, wo, wsem.at[0])
    load_wq = pltpu.make_async_copy(w_qkv, wq, wsem.at[1])
    load_wo.start()
    load_wq.start()
    over_dp = [(dx, dy) for dx in range(4) for dy in range(4) if dx + dy > 0]
    barrier = pltpu.get_barrier_semaphore()
    met = [at.over_xy(dx, dy) for dx, dy in over_dp] + [at.along_m(k) for k in range(1, 8)]
    for device in met:
        pl.semaphore_signal(barrier, inc=1, device_id=device, device_id_type=MESH)

    group_row = dest_group[...]
    member = (lax.broadcasted_iota(jnp.int32, (16, rows), 0) == group_row).astype(F32)
    before = (
        lax.broadcasted_iota(jnp.int32, (rows, rows), 0) < lax.broadcasted_iota(jnp.int32, (rows, rows), 1)
    ).astype(BF16)
    rank = jnp.sum(jnp.dot(member.astype(BF16), before, preferred_element_type=F32) * member, 0, keepdims=True)
    slot = group_row.astype(F32) * 32.0 + rank
    pick = (lax.broadcasted_iota(jnp.int32, (512, rows), 0).astype(F32) == slot).astype(BF16)
    st_pad[...] = jnp.zeros_like(st_pad)
    st_pad[0:1, :] = dest_row[...].astype(F32) + 1.0
    st_pad[1:2, :] = segment[...].astype(F32)
    places[...] = st_pad[...].T
    address = jnp.broadcast_to(places[:, 0:1], (rows, 128)).astype(BF16)
    outbox[:, 0:width] = jnp.dot(pick, patches[...], preferred_element_type=F32).astype(BF16)
    outbox[:, width:] = jnp.dot(pick, address, preferred_element_type=F32).astype(BF16)
    cot_full[m] = cot[...]
    pl.semaphore_wait(barrier, len(met))

    here = pl.ds(pl.multiple_of(g * 32, 32), 32)
    routes = []
    for i, (dx, dy) in enumerate(over_dp):
        device = at.over_xy(dx, dy)
        there = pl.ds(pl.multiple_of(device[0] * 32, 32), 32)
        routes.append(remote(outbox.at[there, :], inbox.at[here, :], rs.at[i], rr.at[i], device))
    for copy in routes:
        copy.start()
    inbox[here, :] = outbox[here, :]

    class Collect:
        def __init__(self, full, z_send, z_recv, b_send, b_recv):
            self.full, self.b_send, self.b_recv = full, b_send, b_recv
            self.z = [
                remote(full.at[m], full.at[m], z_send.at[k - 1], z_recv.at[k - 1], at.along_z(k)) for k in (1, 2, 3)
            ]
            self.b = [self.across(k) for k in range(4)]

        def across(self, k):
            s = self.mine(k)
            return remote(self.full.at[s], self.full.at[s], self.b_send.at[k], self.b_recv.at[k], at.sibling())

        def mine(self, k):
            return ((z + 4 - k) % 4) * 2 + c

        def others(self, k):
            return ((z + 4 - k) % 4) * 2 + 1 - c

        def start(self):
            for k in (1, 3, 2):
                self.z[k - 1].start()
            self.b[0].start()

        def arrive(self, k):
            if k > 0:
                self.z[k - 1].wait_recv()
                self.b[k].start()

        def arrive_other(self, k):
            self.b[k].wait_recv()

        def finish(self):
            for copy in self.z + self.b:
                copy.wait_send()

    mine = pl.ds(pl.multiple_of(a * rows, rows), rows)

    def spread_slab(full, s, buf, send, recv, near):
        for h in (0, 1):
            bx, by = (2 * s + h) // 4, (2 * s + h) % 4
            q, j = bx * (1 - c) + by * c, bx * c + by * (1 - c)
            k = (q - a + 4) % 4
            n = (k + 3) % 4
            src = full.at[s, :, pl.ds(h * half, half)]
            dst = buf.at[mine, pl.ds(pl.multiple_of(j * half, half), half)]

            @pl.when(k == 0)
            def _():
                pltpu.make_async_copy(src, dst, near.at[j]).start()

            @pl.when(k != 0)
            def _():
                remote(src, dst, send.at[n, j], recv.at[n, j], at.along_a(k)).start()

    def spread_ends(full, buf, send, recv, near):
        far = [
            remote(full.at[0, :, 0:half], buf.at[mine, 0:half], send.at[k - 1, j], recv.at[k - 1, j], at.along_a(k))
            for k in (1, 2, 3)
            for j in range(4)
        ]
        local = [pltpu.make_async_copy(full.at[0, :, 0:half], buf.at[mine, 0:half], near.at[j]) for j in range(4)]
        return far, local

    def shard_rows(s):
        return pl.ds(pl.multiple_of(s * width, width), width)

    cots = Collect(cot_full, cz, czr, cb, cbr)
    cots.start()
    load_wo.wait()

    def add_heads(s, first=False):
        term = jnp.dot(cot_full[s], wo[shard_rows(s), :], preferred_element_type=F32)
        d_heads[...] = term if first else d_heads[...] + term

    add_heads(m, True)
    cots.arrive_other(0)
    add_heads(cots.others(0))
    for k in (1, 3):
        cots.arrive(k)
        add_heads(cots.mine(k))
        cots.arrive_other(k)
        add_heads(cots.others(k))

    for copy in routes:
        copy.wait()
    arrived = inbox[:, width : width + 1].astype(F32)
    put = (lax.broadcasted_iota(jnp.int32, (512, rows), 1).astype(F32) + 1.0 == arrived).astype(BF16)
    block = tn_dot(put, inbox[:, 0:width])
    packed[...] = block.astype(BF16)

    def exchange(first, second, out, into, send, recv):
        lane = lax.broadcasted_iota(jnp.int32, (rows, 128), 1)
        out[...] = jnp.where(lane == 0, first, jnp.where(lane == 1, second, 0.0)).T[0:8]
        return [remote(out, into.at[k - 1], send.at[k - 1], recv.at[k - 1], at.along_m(k)) for k in range(1, 8)]

    part_mean = jnp.mean(block, -1, keepdims=True)
    part_center = block - part_mean
    stats = exchange(part_mean, jnp.sum(part_center * part_center, -1, keepdims=True), st_out, st_in, sts, str_)
    for copy in stats:
        copy.start()

    for k in (0, 1, 3):
        spread_slab(cot_full, cots.mine(k), cot_a, cs, cr, cl)
        spread_slab(cot_full, cots.others(k), cot_a, cs, cr, cl)
    for copy in stats:
        copy.wait()
    parts = [st_out[...]] + [st_in[k] for k in range(7)]
    mean = sum(part[0:1] for part in parts) * 0.125
    spread = sum(part[1:2] + width * (part[0:1] - mean) * (part[0:1] - mean) for part in parts)
    st_pad[0:1, :] = mean
    st_pad[1:2, :] = lax.rsqrt(spread * (1.0 / 6144.0) + 1e-06)
    columns[...] = st_pad[...].T
    gain_part = gain[:, pl.ds(pl.multiple_of(m * width, width), width)]
    unit = (packed[...].astype(F32) - columns[:, 0:1]) * columns[:, 1:2]
    normed_full[m] = (unit * gain_part).astype(BF16)
    norms = Collect(normed_full, nz, nzr, nb, nbr)
    norms.start()

    cots.arrive(2)
    spread_slab(cot_full, cots.mine(2), cot_a, cs, cr, cl)
    add_heads(cots.mine(2))
    cots.arrive_other(2)
    spread_slab(cot_full, cots.others(2), cot_a, cs, cr, cl)
    add_heads(cots.others(2))
    load_wq.wait()

    def add_projected(s, first=False):
        spread_slab(normed_full, s, normed_a, ns, nr, nl)
        for t in range(3):
            cols = slice(t * half, (t + 1) * half)
            term = jnp.dot(normed_full[s], wq[t, shard_rows(s), :], preferred_element_type=F32)
            proj[:, cols] = term if first else proj[:, cols] + term

    add_projected(m, True)
    norms.arrive_other(0)
    add_projected(norms.others(0))
    for k in (1, 3, 2):
        norms.arrive(k)
        add_projected(norms.mine(k))
        norms.arrive_other(k)
        add_projected(norms.others(k))

    same = places[:, 1:2] == segment[...].astype(F32)

    def normalise(values):
        center = values - jnp.mean(values, -1, keepdims=True)
        inverse = lax.rsqrt(jnp.mean(center * center, -1, keepdims=True) + 1e-06)
        return center * inverse, inverse

    def normalise_back(grad, unit, inverse, weight):
        scaled = grad.astype(BF16).astype(F32) * weight
        inner = scaled - jnp.mean(scaled, -1, keepdims=True) - unit * jnp.mean(scaled * unit, -1, keepdims=True)
        return (inverse * inner).astype(BF16)

    root = DH ** (-0.5)
    for h in range(3):
        q_cols, k_cols, v_cols = (slice(t * half + h * DH, t * half + (h + 1) * DH) for t in range(3))
        h_cols = slice(h * DH, (h + 1) * DH)
        unit_q, inverse_q = normalise(proj[:, q_cols])
        unit_k, inverse_k = normalise(proj[:, k_cols])
        queries = (unit_q * qk_gain[0:1, :]).astype(BF16)
        keys = (unit_k * qk_gain[1:2, :]).astype(BF16)
        values = proj[:, v_cols].astype(BF16)
        raised = jnp.where(same, jnp.exp(nt_dot(queries, keys) * root), 0.0)
        exact = raised / jnp.sum(raised, -1, keepdims=True)
        weights = exact.astype(BF16)
        heads[:, h_cols] = jnp.dot(weights, values, preferred_element_type=F32).astype(BF16)
        given = d_heads[:, h_cols].astype(BF16)
        d_weights = nt_dot(given, values).astype(BF16).astype(F32)
        dproj[:, v_cols] = tn_dot(weights, given).astype(BF16)
        inner = jnp.sum(d_weights * exact, -1, keepdims=True)
        d_scores = (exact * (d_weights - inner) * root).astype(BF16)
        d_queries = jnp.dot(d_scores, keys, preferred_element_type=F32)
        d_keys = tn_dot(d_scores, queries)
        dproj[:, q_cols] = normalise_back(d_queries, unit_q, inverse_q, qk_gain[0:1, :])
        dproj[:, k_cols] = normalise_back(d_keys, unit_k, inverse_k, qk_gain[1:2, :])

    def gather(part, buf, send, recv):
        return [remote(part, buf.at[mine, :], send.at[k - 1], recv.at[k - 1], at.along_a(k)) for k in (1, 2, 3)]

    heads_copies = gather(heads, heads_a, hs, hr)
    dproj_copies = gather(dproj, dproj_a, ps, pr)
    for copy in heads_copies + dproj_copies:
        copy.start()
    heads_a[mine, :] = heads[...]
    dproj_a[mine, :] = dproj[...]
    cots.finish()
    cot_far, cot_near = spread_ends(cot_full, cot_a, cs, cr, cl)
    for copy in cot_far:
        copy.wait_send()
    for copy in cot_near:
        copy.wait()

    sib_out, z_out = cot_full.at[0:4], cot_full.at[4:7]
    def attn_term(shard):
        rows = shard_rows(shard)
        return nt_dot(heads[...], wo[rows, :])

    def dn_term(shard):
        rows = shard_rows(shard)
        total = nt_dot(dproj[:, 0:half], wq[0, rows, :])
        total += nt_dot(dproj[:, half : 2 * half], wq[1, rows, :])
        return total + nt_dot(dproj[:, 2 * half : 3 * half], wq[2, rows, :])

    def to_sibling(term, out, into, send, recv):
        def step(k, carry):
            out[k] = term(((z + 1 + k) % 4) * 2 + 1 - c).astype(BF16)
            remote(out.at[k], into.at[k], send.at[k], recv.at[k], at.sibling()).start()
            return carry

        lax.fori_loop(0, 4, step, 0)

    def along_z(term, sib_o, sib, sib_send, sib_recv, out, into, send, recv, own):
        def step(k, carry):
            value = term(((z + 1 + k) % 4) * 2 + c)
            remote(sib_o.at[k], sib.at[k], sib_send.at[k], sib_recv.at[k], at.sibling()).wait()
            out[k] = (value + sib[k].astype(F32)).astype(BF16)
            remote(out.at[k], into.at[k], send.at[k], recv.at[k], at.along_z(1 + k)).start()
            return carry

        lax.fori_loop(0, 3, step, 0)
        value = term(z * 2 + c)
        remote(sib_o.at[3], sib.at[3], sib_send.at[3], sib_recv.at[3], at.sibling()).wait()
        own[...] = value + sib[3].astype(F32)

    to_sibling(attn_term, sib_out, sib_in, ss, sr)
    to_sibling(dn_term, dn_sib_out, dn_sib_in, dss, dsr)
    along_z(attn_term, sib_out, sib_in, ss, sr, z_out, z_in, zs, zr, own_at)
    along_z(dn_term, dn_sib_out, dn_sib_in, dss, dsr, dn_z_out, dn_z_in, dzs, dzr, own_dn)

    for copy in heads_copies:
        copy.wait()
    for copy in cot_far:
        copy.wait_recv()

    og_out = [wo.at[pl.ds(3456 + half * k, half), :] for k in range(3)]
    qg_out = [wo.at[pl.ds(1152 * k, 1152), :] for k in range(3)]

    def out_term(j):
        return tn_dot(cot_a[:, pl.ds(pl.multiple_of(j * half, half), half)], heads_a[...])

    og_copies = [remote(og_out[k], og_in.at[k], os_.at[k], or_.at[k], at.along_b(1 + k)) for k in range(3)]
    qg_copies = [remote(qg_out[k], qg_in.at[k], qs.at[k], qr.at[k], at.along_b(1 + k)) for k in range(3)]

    def out_step(k, carry):
        to = pl.ds(pl.multiple_of(3456 + half * k, half), half)
        wo[to, :] = out_term((b + 1 + k) % 4).astype(BF16)
        remote(wo.at[to, :], og_in.at[k], os_.at[k], or_.at[k], at.along_b(1 + k)).start()
        return carry

    lax.fori_loop(0, 3, out_step, 0)
    own_og[...] = out_term(b)

    norms.finish()
    normed_far, normed_near = spread_ends(normed_full, normed_a, ns, nr, nl)
    for copy in dproj_copies + normed_far + normed_near:
        copy.wait()

    def qkv_term(j):
        return tn_dot(normed_a[:, pl.ds(pl.multiple_of(j * half, half), half)], dproj_a[...])

    def qkv_step(k, carry):
        term = qkv_term((b + 1 + k) % 4).astype(BF16)
        for t in range(3):
            wo[pl.ds(pl.multiple_of(1152 * k + half * t, half), half), :] = term[:, t * half : (t + 1) * half]
        to = pl.ds(pl.multiple_of(1152 * k, half), 1152)
        remote(wo.at[to, :], qg_in.at[k], qs.at[k], qr.at[k], at.along_b(1 + k)).start()
        return carry

    lax.fori_loop(0, 3, qkv_step, 0)
    own_qg[...] = qkv_term(b)

    total = own_at[...]
    for k in range(3):
        remote(z_out.at[k], z_in.at[k], zs.at[k], zr.at[k], at.along_z(1 + k)).wait()
        total += z_in[k].astype(F32)
    output[...] = (packed[...].astype(F32) + total).astype(BF16)

    total = own_dn[...]
    for k in range(3):
        remote(dn_z_out.at[k], dn_z_in.at[k], dzs.at[k], dzr.at[k], at.along_z(1 + k)).wait()
        total += dn_z_in[k].astype(F32)
    rstd = columns[:, 1:2]
    unit = (packed[...].astype(F32) - columns[:, 0:1]) * rstd
    u = total * gain_part
    own_dn[...] = u
    ends = exchange(jnp.sum(u, -1, keepdims=True), jnp.sum(u * unit, -1, keepdims=True), en_out, en_in, ens, enr)
    for copy in ends:
        copy.start()
    for copy in ends:
        copy.wait()
    st_pad[0:8, :] = (en_out[...] + sum(en_in[k] for k in range(7))) * (1.0 / 6144.0)
    means = st_pad[...].T
    unit = (packed[...].astype(F32) - columns[:, 0:1]) * rstd
    grad = rstd * (own_dn[...] - means[:, 0:1] - unit * means[:, 1:2])
    input_grad[...] = (cot[...].astype(F32) + grad).astype(BF16)

    for copy in og_copies:
        copy.wait()
    out_grad[...] = ((own_og[...] + sum(og_in[k].astype(F32) for k in range(3))) * scale).astype(BF16)
    for copy in qg_copies:
        copy.wait()
    for t in range(3):
        part = slice(t * half, (t + 1) * half)
        total = own_qg[:, part] + sum(qg_in[k, part, :].astype(F32) for k in range(3))
        qkv_grad[t] = (total * scale).astype(BF16)


def shards(patches, dest_group, dest_row, segment, ln_gain, w_qkv, qk_gain, w_out, cotangent):
    vmem = pl.BlockSpec(memory_space=pltpu.VMEM)
    anywhere = pl.BlockSpec(memory_space=pl.ANY)
    dma = pltpu.SemaphoreType.DMA
    V = pltpu.VMEM
    scale = 1.0 / math.sqrt(4096)
    output, input_grad, qkv_grad, out_grad = pl.pallas_call(
        functools.partial(whole, scale),
        out_shape=(
            jax.ShapeDtypeStruct((256, 768), BF16),
            jax.ShapeDtypeStruct((256, 768), BF16),
            jax.ShapeDtypeStruct((3, 384, 384), BF16),
            jax.ShapeDtypeStruct((384, 384), BF16),
        ),
        in_specs=[vmem, vmem, vmem, vmem, vmem, anywhere, vmem, anywhere, vmem],
        out_specs=(vmem,) * 4,
        scratch_shapes=[
            V((512, 896), BF16), V((512, 896), BF16), V((256, 768), BF16),
            V((8, 256, 768), BF16), V((8, 256, 768), BF16),
            V((1024, 1536), BF16), V((1024, 1536), BF16), V((1024, 384), BF16), V((1024, 1152), BF16),
            V((3, 6144, 384), BF16), V((6144, 384), BF16),
            V((256, 1152), F32), V((256, 384), F32), V((256, 384), BF16), V((256, 1152), BF16),
            V((256, 128), F32), V((256, 128), F32), V((128, 256), F32),
            V((8, 256), F32), V((7, 8, 256), F32), V((8, 256), F32), V((7, 8, 256), F32),
            V((4, 256, 768), BF16), V((3, 256, 768), BF16),
            V((4, 256, 768), BF16), V((4, 256, 768), BF16), V((3, 256, 768), BF16), V((3, 256, 768), BF16),
            V((3, 384, 384), BF16), V((3, 1152, 384), BF16),
            V((384, 384), F32), V((384, 1152), F32), V((256, 768), F32), V((256, 768), F32),
            dma((2,)), dma((15,)), dma((15,)),
            dma((3,)), dma((3,)), dma((4,)), dma((4,)), dma((3,)), dma((3,)), dma((4,)), dma((4,)),
            dma((7,)), dma((7,)), dma((7,)), dma((7,)),
            dma((3, 4)), dma((3, 4)), dma((4,)), dma((3, 4)), dma((3, 4)), dma((4,)),
            dma((3,)), dma((3,)), dma((3,)), dma((3,)),
            dma((4,)), dma((4,)), dma((3,)), dma((3,)), dma((4,)), dma((4,)), dma((3,)), dma((3,)),
            dma((3,)), dma((3,)), dma((3,)), dma((3,)),
        ],
        compiler_params=pltpu.CompilerParams(
            collective_id=1, has_side_effects=True, vmem_limit_bytes=62 << 20
        ),
        name="whole",
    )(
        patches, dest_group.reshape(1, 256), dest_row.reshape(1, 256), segment.reshape(1, 256),
        ln_gain.reshape(1, 6144), jnp.transpose(w_qkv, (1, 0, 2)), qk_gain, w_out, cotangent,
    )
    return (output, input_grad, jnp.transpose(qkv_grad, (1, 0, 2)), out_grad)


def solution(mesh):
    placed = (
        P("dp", "mp"),
        P("dp"),
        P("dp"),
        P("dp"),
        P(),
        P(None, None, "mp"),
        P(),
        P(None, "mp"),
        P("dp", "mp"),
    )
    return jax.shard_map(
        shards,
        mesh=mesh,
        in_specs=placed,
        out_specs=(P("dp", "mp"), P("dp", "mp"), P("dp", None, "mp"), P("dp", "mp")),
        check_vma=False,
    )
```

time: 201 us -> 151 us (0.75)
  the two profiles are of different devices: /device:TPU:1 before, /device:TPU:64 now
where the time goes in v2:
time: 151 us; the launch traced here: 150 us
  Pallas kernels  142 us (94%)
  local copies, waits for them, and re-layouts  7.4 us (5%)
    pallas_call x1, Pallas kernels, shards(): pl.pallas_call(functools.partial(whole, scale), out_shape=(jax.ShapeDtype...  142 us
    unnamed x4, local copies, waits for them, and re-layouts  7.4 us

profile of v2, /device:TPU:64, one launch (start us, length us, event | category | flops | bytes accessed | tf_op | source)
XLA Modules:
  0.0 150.5 jit_solution(5050190633275248434)
XLA Ops:
  0.6 142.4 %whole.1 = (bf16[256,768]{1,0:T(8,128)(2,1)}, bf16[256,768]{1,0:T(8,128)(2,1)}, bf16[3,384,384]{2,1,0:T(8,128)(2,1)}, bf16[384,384]{1,0:T(8,128)(2,1)}) custom-call(bf16[256,768]{1,0:T(8,128)(2,1)} %patches.1, s32[1,256]{1,0:T(1,128)} %bitcast.9, s32[1,256]{1,0:T(1,128)} %bitcast.10, s32[1,256]{1,0:T(1,128)} %bitcast.11, f32[1,6144]{1,0:T(1,128)} %bitcast.8, ...), custom_call_target="tpu_custom_call" | custom-call | tf_op jit(solution)/shard_map/whole/pallas_call | solution.py:431
  143.1 1.8 %copy.17 = bf16[256,768]{1,0:T(8,128)(2,1)} copy(bf16[256,768]{1,0:T(8,128)(2,1)} %get-tuple-element.16) | data formatting | bytes 786432
  144.8 1.8 %copy.18 = bf16[256,768]{1,0:T(8,128)(2,1)} copy(bf16[256,768]{1,0:T(8,128)(2,1)} %get-tuple-element.17) | data formatting | bytes 786432
  146.6 2.2 %copy.19 = bf16[384,3,384]{2,0,1:T(8,128)(2,1)} copy(bf16[384,3,384]{2,0,1:T(8,128)(2,1)} %bitcast.7) | data formatting | bytes 1769472
  148.8 1.7 %copy.20 = bf16[384,384]{1,0:T(8,128)(2,1)} copy(bf16[384,384]{1,0:T(8,128)(2,1)} %get-tuple-element.19) | data formatting | bytes 589824

commit v3 on v2

--- a/solution.py
+++ b/solution.py
@@ -66,12 +66,12 @@
     scale,
     patches, dest_group, dest_row, segment, gain, w_qkv, qk_gain, w_out, cot,
     output, input_grad, qkv_grad, out_grad,
-    outbox, inbox, packed, cot_full, normed_full, cot_a, normed_a, heads_a, dproj_a, wq, wo,
+    outbox, inbox, packed, cot_full, normed_full, cot_a, normed_a, parts_a, wq, wo,
     proj, d_heads, heads, dproj, columns, places, st_pad, st_out, st_in, en_out, en_in,
-    sib_in, z_in, dn_sib_out, dn_sib_in, dn_z_out, dn_z_in, og_in, qg_in,
-    own_og, own_qg, own_at, own_dn,
+    sib_in, z_in, dn_sib_out, dn_sib_in, dn_z_out, dn_z_in, far_in, near_in,
+    own_part, own_at, own_dn,
     wsem, rs, rr, cz, czr, cb, cbr, nz, nzr, nb, nbr, sts, str_, ens, enr,
-    cs, cr, cl, ns, nr, nl, hs, hr, ps, pr, ss, sr, zs, zr, dss, dsr, dzs, dzr, os_, or_, qs, qr,
+    cs, cr, cl, ns, nr, nl, gs, gr, ss, sr, zs, zr, dss, dsr, dzs, dzr, qs, qr,
 ):
     at = Place()
     a, b, c, z, m, g = at.a, at.b, at.c, at.z, at.m, at.g
@@ -116,15 +116,14 @@
 
     class Collect:
         def __init__(self, full, z_send, z_recv, b_send, b_recv):
-            self.full, self.b_send, self.b_recv = full, b_send, b_recv
+            up, down = at.along_z(1), at.along_z(3)
+            own, low, high = full.at[m], full.at[self.mine(1), 0:128, :], full.at[self.mine(3), 128:256, :]
             self.z = [
-                remote(full.at[m], full.at[m], z_send.at[k - 1], z_recv.at[k - 1], at.along_z(k)) for k in (1, 2, 3)
+                remote(src, src, z_send.at[i], z_recv.at[i], to)
+                for i, (src, to) in enumerate([(own, up), (own, down), (low, up), (high, down)])
             ]
-            self.b = [self.across(k) for k in range(4)]
-
-        def across(self, k):
-            s = self.mine(k)
-            return remote(self.full.at[s], self.full.at[s], self.b_send.at[k], self.b_recv.at[k], at.sibling())
+            slabs = [full.at[self.mine(k)] for k in range(4)]
+            self.b = [remote(slabs[k], slabs[k], b_send.at[k], b_recv.at[k], at.sibling()) for k in range(4)]
 
         def mine(self, k):
             return ((z + 4 - k) % 4) * 2 + c
@@ -133,14 +132,18 @@
             return ((z + 4 - k) % 4) * 2 + 1 - c
 
         def start(self):
-            for k in (1, 3, 2):
-                self.z[k - 1].start()
+            self.z[0].start()
+            self.z[1].start()
             self.b[0].start()
 
         def arrive(self, k):
-            if k > 0:
-                self.z[k - 1].wait_recv()
-                self.b[k].start()
+            if k == 2:
+                self.z[2].wait_recv()
+                self.z[3].wait_recv()
+            else:
+                self.z[k // 2].wait_recv()
+                self.z[2 + k // 2].start()
+            self.b[k].start()
 
         def arrive_other(self, k):
             self.b[k].wait_recv()
@@ -191,8 +194,9 @@
     add_heads(m, True)
     cots.arrive_other(0)
     add_heads(cots.others(0))
+    cots.arrive(1)
+    cots.arrive(3)
     for k in (1, 3):
-        cots.arrive(k)
         add_heads(cots.mine(k))
         cots.arrive_other(k)
         add_heads(cots.others(k))
@@ -250,11 +254,16 @@
     add_projected(m, True)
     norms.arrive_other(0)
     add_projected(norms.others(0))
-    for k in (1, 3, 2):
-        norms.arrive(k)
+    norms.arrive(1)
+    norms.arrive(3)
+    for k in (1, 3):
         add_projected(norms.mine(k))
         norms.arrive_other(k)
         add_projected(norms.others(k))
+    norms.arrive(2)
+    add_projected(norms.mine(2))
+    norms.arrive_other(2)
+    add_projected(norms.others(2))
 
     same = places[:, 1:2] == segment[...].astype(F32)
 
@@ -291,15 +300,73 @@
         dproj[:, q_cols] = normalise_back(d_queries, unit_q, inverse_q, qk_gain[0:1, :])
         dproj[:, k_cols] = normalise_back(d_keys, unit_k, inverse_k, qk_gain[1:2, :])
 
-    def gather(part, buf, send, recv):
-        return [remote(part, buf.at[mine, :], send.at[k - 1], recv.at[k - 1], at.along_a(k)) for k in (1, 2, 3)]
-
-    heads_copies = gather(heads, heads_a, hs, hr)
-    dproj_copies = gather(dproj, dproj_a, ps, pr)
-    for copy in heads_copies + dproj_copies:
-        copy.start()
-    heads_a[mine, :] = heads[...]
-    dproj_a[mine, :] = dproj[...]
+    for part in range(4):
+        block = heads[...] if part == 0 else dproj[:, (part - 1) * half : part * half]
+        parts_a[part, :, mine] = block.T
+
+    def window(part, k, lines):
+        cols = pl.ds(pl.multiple_of(((a + k) % 4) * rows, rows), rows)
+        return parts_a.at[part, lines, cols]
+
+    low, high, every = slice(0, 192), slice(192, 384), slice(0, 384)
+    gathers = []
+    for part in range(4):
+        hops = [(0, every, 1), (0, every, 3), (3, low, 1), (1, high, 3)]
+        refs = [(window(part, k, lines), at.along_a(to)) for k, lines, to in hops]
+        gathers.append([remote(src, src, gs.at[part, i], gr.at[part, i], to) for i, (src, to) in enumerate(refs)])
+    for part in range(4):
+        gathers[part][0].start()
+        gathers[part][1].start()
+
+    def relay(part):
+        for i in (0, 1):
+            gathers[part][i].wait_recv()
+            gathers[part][i + 2].start()
+
+    def gathered(part):
+        gathers[part][2].wait_recv()
+        gathers[part][3].wait_recv()
+
+    def held(part, i):
+        return slice((3 * part + i) * half, (3 * part + i + 1) * half)
+
+    def product(part, k):
+        left = cot_a if part == 0 else normed_a
+        cols = pl.ds(pl.multiple_of(((b + k) % 4) * half, half), half)
+        return jnp.dot(parts_a[part], left[:, cols], preferred_element_type=F32)
+
+    sums = []
+    for part in range(4):
+        far, after, ahead = (wo.at[held(part, i), :] for i in range(3))
+        pairs = [
+            (far.at[low, :], far_in.at[part, low, :], 1),
+            (far.at[high, :], far_in.at[part, high, :], 3),
+            (after, near_in.at[part, 0], 1),
+            (ahead, near_in.at[part, 1], 3),
+        ]
+        sums.append([remote(src, dst, qs.at[part, i], qr.at[part, i], at.along_b(to)) for i, (src, dst, to) in enumerate(pairs)])
+
+    def send_far(part):
+        wo[held(part, 0), :] = product(part, 2).astype(BF16)
+        sums[part][0].start()
+        sums[part][1].start()
+
+    def send_near(part):
+        for i, k in enumerate((1, 3)):
+            own_part[part] = product(part, k)
+            sums[part][i].wait_recv()
+            lines = (low, high)[i]
+            own_part[part, lines, :] += far_in[part, lines, :].astype(F32)
+            wo[held(part, 1 + i), :] = own_part[part].astype(BF16)
+            sums[part][2 + i].start()
+        own_part[part] = product(part, 0)
+
+    def total_of(part):
+        for i in (2, 3):
+            sums[part][i].wait_recv()
+        total = own_part[part] + near_in[part, 0].astype(F32) + near_in[part, 1].astype(F32)
+        return (total * scale).T.astype(BF16)
+
     cots.finish()
     cot_far, cot_near = spread_ends(cot_full, cot_a, cs, cr, cl)
     for copy in cot_far:
@@ -340,51 +407,28 @@
         own[...] = value + sib[3].astype(F32)
 
     to_sibling(attn_term, sib_out, sib_in, ss, sr)
+    relay(0)
     to_sibling(dn_term, dn_sib_out, dn_sib_in, dss, dsr)
+    relay(1)
     along_z(attn_term, sib_out, sib_in, ss, sr, z_out, z_in, zs, zr, own_at)
-    along_z(dn_term, dn_sib_out, dn_sib_in, dss, dsr, dn_z_out, dn_z_in, dzs, dzr, own_dn)
-
-    for copy in heads_copies:
-        copy.wait()
     for copy in cot_far:
         copy.wait_recv()
-
-    og_out = [wo.at[pl.ds(3456 + half * k, half), :] for k in range(3)]
-    qg_out = [wo.at[pl.ds(1152 * k, 1152), :] for k in range(3)]
-
-    def out_term(j):
-        return tn_dot(cot_a[:, pl.ds(pl.multiple_of(j * half, half), half)], heads_a[...])
-
-    og_copies = [remote(og_out[k], og_in.at[k], os_.at[k], or_.at[k], at.along_b(1 + k)) for k in range(3)]
-    qg_copies = [remote(qg_out[k], qg_in.at[k], qs.at[k], qr.at[k], at.along_b(1 + k)) for k in range(3)]
-
-    def out_step(k, carry):
-        to = pl.ds(pl.multiple_of(3456 + half * k, half), half)
-        wo[to, :] = out_term((b + 1 + k) % 4).astype(BF16)
-        remote(wo.at[to, :], og_in.at[k], os_.at[k], or_.at[k], at.along_b(1 + k)).start()
-        return carry
-
-    lax.fori_loop(0, 3, out_step, 0)
-    own_og[...] = out_term(b)
-
+    gathered(0)
+    send_far(0)
+    relay(2)
+    along_z(dn_term, dn_sib_out, dn_sib_in, dss, dsr, dn_z_out, dn_z_in, dzs, dzr, own_dn)
+    relay(3)
+    send_near(0)
     norms.finish()
     normed_far, normed_near = spread_ends(normed_full, normed_a, ns, nr, nl)
-    for copy in dproj_copies + normed_far + normed_near:
+    for copy in normed_far + normed_near:
         copy.wait()
-
-    def qkv_term(j):
-        return tn_dot(normed_a[:, pl.ds(pl.multiple_of(j * half, half), half)], dproj_a[...])
-
-    def qkv_step(k, carry):
-        term = qkv_term((b + 1 + k) % 4).astype(BF16)
-        for t in range(3):
-            wo[pl.ds(pl.multiple_of(1152 * k + half * t, half), half), :] = term[:, t * half : (t + 1) * half]
-        to = pl.ds(pl.multiple_of(1152 * k, half), 1152)
-        remote(wo.at[to, :], qg_in.at[k], qs.at[k], qr.at[k], at.along_b(1 + k)).start()
-        return carry
-
-    lax.fori_loop(0, 3, qkv_step, 0)
-    own_qg[...] = qkv_term(b)
+    for part in (1, 2, 3):
+        gathered(part)
+        send_far(part)
+        if part > 1:
+            send_near(part - 1)
+    send_near(3)
 
     total = own_at[...]
     for k in range(3):
@@ -411,15 +455,21 @@
     grad = rstd * (own_dn[...] - means[:, 0:1] - unit * means[:, 1:2])
     input_grad[...] = (cot[...].astype(F32) + grad).astype(BF16)
 
-    for copy in og_copies:
+    out_grad[...] = total_of(0)
+    for t in range(3):
+        qkv_grad[t] = total_of(1 + t)
+    for part in range(4):
+        for copy in gathers[part] + sums[part]:
+            copy.wait_send()
+
+
+def hand_over(*refs):
+    sources, results, sem = refs[:4], refs[4:8], refs[8]
+    copies = [pltpu.make_async_copy(src, dst, sem.at[i]) for i, (src, dst) in enumerate(zip(sources, results))]
+    for copy in copies:
+        copy.start()
+    for copy in copies:
         copy.wait()
-    out_grad[...] = ((own_og[...] + sum(og_in[k].astype(F32) for k in range(3))) * scale).astype(BF16)
-    for copy in qg_copies:
-        copy.wait()
-    for t in range(3):
-        part = slice(t * half, (t + 1) * half)
-        total = own_qg[:, part] + sum(qg_in[k, part, :].astype(F32) for k in range(3))
-        qkv_grad[t] = (total * scale).astype(BF16)
 
 
 def shards(patches, dest_group, dest_row, segment, ln_gain, w_qkv, qk_gain, w_out, cotangent):
@@ -428,35 +478,36 @@
     dma = pltpu.SemaphoreType.DMA
     V = pltpu.VMEM
     scale = 1.0 / math.sqrt(4096)
-    output, input_grad, qkv_grad, out_grad = pl.pallas_call(
+    out_shape = (
+        jax.ShapeDtypeStruct((256, 768), BF16),
+        jax.ShapeDtypeStruct((256, 768), BF16),
+        jax.ShapeDtypeStruct((3, 384, 384), BF16),
+        jax.ShapeDtypeStruct((384, 384), BF16),
+    )
+    results = pl.pallas_call(
         functools.partial(whole, scale),
-        out_shape=(
-            jax.ShapeDtypeStruct((256, 768), BF16),
-            jax.ShapeDtypeStruct((256, 768), BF16),
-            jax.ShapeDtypeStruct((3, 384, 384), BF16),
-            jax.ShapeDtypeStruct((384, 384), BF16),
-        ),
+        out_shape=out_shape,
         in_specs=[vmem, vmem, vmem, vmem, vmem, anywhere, vmem, anywhere, vmem],
         out_specs=(vmem,) * 4,
         scratch_shapes=[
             V((512, 896), BF16), V((512, 896), BF16), V((256, 768), BF16),
             V((8, 256, 768), BF16), V((8, 256, 768), BF16),
-            V((1024, 1536), BF16), V((1024, 1536), BF16), V((1024, 384), BF16), V((1024, 1152), BF16),
+            V((1024, 1536), BF16), V((1024, 1536), BF16), V((4, 384, 1024), BF16),
             V((3, 6144, 384), BF16), V((6144, 384), BF16),
             V((256, 1152), F32), V((256, 384), F32), V((256, 384), BF16), V((256, 1152), BF16),
             V((256, 128), F32), V((256, 128), F32), V((128, 256), F32),
             V((8, 256), F32), V((7, 8, 256), F32), V((8, 256), F32), V((7, 8, 256), F32),
             V((4, 256, 768), BF16), V((3, 256, 768), BF16),
             V((4, 256, 768), BF16), V((4, 256, 768), BF16), V((3, 256, 768), BF16), V((3, 256, 768), BF16),
-            V((3, 384, 384), BF16), V((3, 1152, 384), BF16),
-            V((384, 384), F32), V((384, 1152), F32), V((256, 768), F32), V((256, 768), F32),
+            V((4, 384, 384), BF16), V((4, 2, 384, 384), BF16),
+            V((4, 384, 384), F32), V((256, 768), F32), V((256, 768), F32),
             dma((2,)), dma((15,)), dma((15,)),
-            dma((3,)), dma((3,)), dma((4,)), dma((4,)), dma((3,)), dma((3,)), dma((4,)), dma((4,)),
+            dma((4,)), dma((4,)), dma((4,)), dma((4,)), dma((4,)), dma((4,)), dma((4,)), dma((4,)),
             dma((7,)), dma((7,)), dma((7,)), dma((7,)),
             dma((3, 4)), dma((3, 4)), dma((4,)), dma((3, 4)), dma((3, 4)), dma((4,)),
-            dma((3,)), dma((3,)), dma((3,)), dma((3,)),
+            dma((4, 4)), dma((4, 4)),
             dma((4,)), dma((4,)), dma((3,)), dma((3,)), dma((4,)), dma((4,)), dma((3,)), dma((3,)),
-            dma((3,)), dma((3,)), dma((3,)), dma((3,)),
+            dma((4, 4)), dma((4, 4)),
         ],
         compiler_params=pltpu.CompilerParams(
             collective_id=1, has_side_effects=True, vmem_limit_bytes=62 << 20
@@ -466,6 +517,14 @@
         patches, dest_group.reshape(1, 256), dest_row.reshape(1, 256), segment.reshape(1, 256),
         ln_gain.reshape(1, 6144), jnp.transpose(w_qkv, (1, 0, 2)), qk_gain, w_out, cotangent,
     )
+    output, input_grad, qkv_grad, out_grad = pl.pallas_call(
+        hand_over,
+        out_shape=out_shape,
+        in_specs=[anywhere] * 4,
+        out_specs=(anywhere,) * 4,
+        scratch_shapes=[dma((4,))],
+        name="hand_over",
+    )(*results)
     return (output, input_grad, jnp.transpose(qkv_grad, (1, 0, 2)), out_grad)
 
 

time: 151 us -> 172 us (1.14)
  the two profiles are of different devices: /device:TPU:64 before, /device:TPU:1 now
where the time goes in v3:
time: 172 us
  Pallas kernels  171 us (99%)
    pallas_call x1, Pallas kernels, shards(): pl.pallas_call(functools.partial(whole, scale), out_shape=out_shape, in_s...  111 us
    pallas_call x1, Pallas kernels, shards(): pl.pallas_call(hand_over, out_shape=out_shape, in_specs=[anywhere] * 4, o...  60.7 us

profile of v3, /device:TPU:1, one launch (start us, length us, event | category | flops | bytes accessed | tf_op | source)
XLA Modules:
  0.0 172.3 jit_solution(13604626969994572494)
XLA Ops:
  0.6 110.8 %whole.1 = (bf16[256,768]{1,0:T(8,128)(2,1)}, bf16[256,768]{1,0:T(8,128)(2,1)}, bf16[3,384,384]{2,1,0:T(8,128)(2,1)}, bf16[384,384]{1,0:T(8,128)(2,1)}) custom-call(bf16[256,768]{1,0:T(8,128)(2,1)} %patches.1, s32[1,256]{1,0:T(1,128)} %bitcast.8, s32[1,256]{1,0:T(1,128)} %bitcast.9, s32[1,256]{1,0:T(1,128)} %bitcast.10, f32[1,6144]{1,0:T(1,128)} %bitcast.7, ...), custom_call_target="tpu_custom_call" | custom-call | tf_op jit(solution)/shard_map/whole/pallas_call | solution.py:487
  111.4 60.7 %hand_over.1 = (bf16[256,768]{1,0:T(8,128)(2,1)}, bf16[256,768]{1,0:T(8,128)(2,1)}, bf16[3,384,384]{2,1,0:T(8,128)(2,1)}, bf16[384,384]{1,0:T(8,128)(2,1)}) custom-call(bf16[256,768]{1,0:T(8,128)(2,1)} %get-tuple-element.12.refs_0_, bf16[256,768]{1,0:T(8,128)(2,1)} %get-tuple-element.13.refs_1_, bf16[3,384,384]{2,1,0:T(8,128)(2,1)} %get-tuple-element.14.refs_2_, ...), custom_call_target="tpu_custom_call" | custom-call | tf_op jit(solution)/shard_map/hand_over/pallas_call | solution.py:520

commit v4 on v3

--- a/solution.py
+++ b/solution.py
@@ -62,15 +62,54 @@
     return lax.dot_general(left, right, (((0,), (0,)), ((), ())), preferred_element_type=F32)
 
 
+class Ring:
+    def __init__(self, term, out, own, far_in, near_in, send, recv, along):
+        size = own.shape[0]
+        self.low, self.high = slice(0, size // 2), slice(size // 2, size)
+        self.term, self.out, self.own, self.far_in, self.near_in = term, out, own, far_in, near_in
+        pairs = [
+            (out[0].at[self.low, :], far_in.at[self.low, :], 1),
+            (out[0].at[self.high, :], far_in.at[self.high, :], 3),
+            (out[1], near_in.at[0], 1),
+            (out[2], near_in.at[1], 3),
+        ]
+        self.copies = [remote(src, dst, send.at[i], recv.at[i], along(to)) for i, (src, dst, to) in enumerate(pairs)]
+
+    def send_far(self):
+        self.out[0][...] = self.term(2).astype(BF16)
+        self.copies[0].start()
+        self.copies[1].start()
+
+    def send_near(self):
+        for i, k in enumerate((1, 3)):
+            self.own[...] = self.term(k)
+            self.copies[i].wait_recv()
+            lines = (self.low, self.high)[i]
+            self.own[lines, :] += self.far_in[lines, :].astype(F32)
+            self.out[1 + i][...] = self.own[...].astype(BF16)
+            self.copies[2 + i].start()
+        self.own[...] = self.term(0)
+
+    def total(self):
+        self.copies[2].wait_recv()
+        self.copies[3].wait_recv()
+        return self.own[...] + self.near_in[0].astype(F32) + self.near_in[1].astype(F32)
+
+    def finish(self):
+        for copy in self.copies:
+            copy.wait_send()
+
+
 def whole(
     scale,
-    patches, dest_group, dest_row, segment, gain, w_qkv, qk_gain, w_out, cot,
-    output, input_grad, qkv_grad, out_grad,
+    patches_in, dest_group_in, dest_row_in, segment_in, gain_in, w_qkv, qk_gain_in, w_out, cot_in,
+    output_to, input_grad_to, qkv_grad_to, out_grad_to,
+    patches, dest_group, dest_row, segment, gain, qk_gain, cot, output, input_grad, qkv_grad, out_grad,
     outbox, inbox, packed, cot_full, normed_full, cot_a, normed_a, parts_a, wq, wo,
     proj, d_heads, heads, dproj, columns, places, st_pad, st_out, st_in, en_out, en_in,
     sib_in, z_in, dn_sib_out, dn_sib_in, dn_z_out, dn_z_in, far_in, near_in,
     own_part, own_at, own_dn,
-    wsem, rs, rr, cz, czr, cb, cbr, nz, nzr, nb, nbr, sts, str_, ens, enr,
+    isem, osem, wsem, rs, rr, cz, czr, cb, cbr, nz, nzr, nb, nbr, sts, str_, ens, enr,
     cs, cr, cl, ns, nr, nl, gs, gr, ss, sr, zs, zr, dss, dsr, dzs, dzr, qs, qr,
 ):
     at = Place()
@@ -78,13 +117,20 @@
     width, half, rows = 768, 384, 256
     load_wo = pltpu.make_async_copy(w_out, wo, wsem.at[0])
     load_wq = pltpu.make_async_copy(w_qkv, wq, wsem.at[1])
-    load_wo.start()
-    load_wq.start()
+    pairs = [
+        (dest_group_in, dest_group), (dest_row_in, dest_row), (segment_in, segment), (patches_in, patches),
+        (cot_in, cot_full.at[m]), (cot_in, cot), (gain_in, gain), (qk_gain_in, qk_gain),
+    ]
+    loads = [pltpu.make_async_copy(src, dst, isem.at[i]) for i, (src, dst) in enumerate(pairs)]
     over_dp = [(dx, dy) for dx in range(4) for dy in range(4) if dx + dy > 0]
     barrier = pltpu.get_barrier_semaphore()
     met = [at.over_xy(dx, dy) for dx, dy in over_dp] + [at.along_m(k) for k in range(1, 8)]
     for device in met:
         pl.semaphore_signal(barrier, inc=1, device_id=device, device_id_type=MESH)
+    for copy in loads + [load_wo, load_wq]:
+        copy.start()
+    for copy in loads[0:4]:
+        copy.wait()
 
     group_row = dest_group[...]
     member = (lax.broadcasted_iota(jnp.int32, (16, rows), 0) == group_row).astype(F32)
@@ -101,7 +147,8 @@
     address = jnp.broadcast_to(places[:, 0:1], (rows, 128)).astype(BF16)
     outbox[:, 0:width] = jnp.dot(pick, patches[...], preferred_element_type=F32).astype(BF16)
     outbox[:, width:] = jnp.dot(pick, address, preferred_element_type=F32).astype(BF16)
-    cot_full[m] = cot[...]
+    for copy in loads[4:]:
+        copy.wait()
     pl.semaphore_wait(barrier, len(met))
 
     here = pl.ds(pl.multiple_of(g * 32, 32), 32)
@@ -117,13 +164,14 @@
     class Collect:
         def __init__(self, full, z_send, z_recv, b_send, b_recv):
             up, down = at.along_z(1), at.along_z(3)
-            own, low, high = full.at[m], full.at[self.mine(1), 0:128, :], full.at[self.mine(3), 128:256, :]
-            self.z = [
-                remote(src, src, z_send.at[i], z_recv.at[i], to)
-                for i, (src, to) in enumerate([(own, up), (own, down), (low, up), (high, down)])
-            ]
-            slabs = [full.at[self.mine(k)] for k in range(4)]
-            self.b = [remote(slabs[k], slabs[k], b_send.at[k], b_recv.at[k], at.sibling()) for k in range(4)]
+            self.z, self.b = [], []
+            for h in (0, 1):
+                part, low, high = (slice(128 * h + i, 128 * h + j) for i, j in ((0, 128), (0, 64), (64, 128)))
+                own = full.at[m, part, :]
+                hops = [(own, up), (own, down), (full.at[self.mine(1), low, :], up), (full.at[self.mine(3), high, :], down)]
+                self.z.append([remote(src, src, z_send.at[h, i], z_recv.at[h, i], to) for i, (src, to) in enumerate(hops)])
+                slabs = [full.at[self.mine(k), part, :] for k in range(4)]
+                self.b.append([remote(slabs[k], slabs[k], b_send.at[h, k], b_recv.at[h, k], at.sibling()) for k in range(4)])
 
         def mine(self, k):
             return ((z + 4 - k) % 4) * 2 + c
@@ -132,52 +180,58 @@
             return ((z + 4 - k) % 4) * 2 + 1 - c
 
         def start(self):
-            self.z[0].start()
-            self.z[1].start()
-            self.b[0].start()
-
-        def arrive(self, k):
-            if k == 2:
-                self.z[2].wait_recv()
-                self.z[3].wait_recv()
-            else:
-                self.z[k // 2].wait_recv()
-                self.z[2 + k // 2].start()
-            self.b[k].start()
-
-        def arrive_other(self, k):
-            self.b[k].wait_recv()
+            for h in (0, 1):
+                self.z[h][0].start()
+                self.z[h][1].start()
+                self.b[h][0].start()
+
+        def near(self, h):
+            for i in (0, 1):
+                self.z[h][i].wait_recv()
+                self.z[h][2 + i].start()
+                self.b[h][1 + 2 * i].start()
+
+        def far(self, h):
+            self.z[h][2].wait_recv()
+            self.z[h][3].wait_recv()
+            self.b[h][2].start()
+
+        def other(self, k, h):
+            self.b[h][k].wait_recv()
 
         def finish(self):
-            for copy in self.z + self.b:
+            for copy in self.z[0] + self.z[1] + self.b[0] + self.b[1]:
                 copy.wait_send()
 
     mine = pl.ds(pl.multiple_of(a * rows, rows), rows)
 
-    def spread_slab(full, s, buf, send, recv, near):
+    def spread_slab(full, s, half_of, buf, send, recv, near):
+        lines = pl.ds(pl.multiple_of(a * rows + 128 * half_of, 128), 128)
         for h in (0, 1):
             bx, by = (2 * s + h) // 4, (2 * s + h) % 4
             q, j = bx * (1 - c) + by * c, bx * c + by * (1 - c)
             k = (q - a + 4) % 4
             n = (k + 3) % 4
-            src = full.at[s, :, pl.ds(h * half, half)]
-            dst = buf.at[mine, pl.ds(pl.multiple_of(j * half, half), half)]
+            src = full.at[s, 128 * half_of : 128 * half_of + 128, pl.ds(h * half, half)]
+            dst = buf.at[lines, pl.ds(pl.multiple_of(j * half, half), half)]
 
             @pl.when(k == 0)
             def _():
-                pltpu.make_async_copy(src, dst, near.at[j]).start()
+                pltpu.make_async_copy(src, dst, near.at[half_of, j]).start()
 
             @pl.when(k != 0)
             def _():
-                remote(src, dst, send.at[n, j], recv.at[n, j], at.along_a(k)).start()
+                remote(src, dst, send.at[half_of, n, j], recv.at[half_of, n, j], at.along_a(k)).start()
 
     def spread_ends(full, buf, send, recv, near):
+        src, dst = full.at[0, 0:128, 0:half], buf.at[0:128, 0:half]
         far = [
-            remote(full.at[0, :, 0:half], buf.at[mine, 0:half], send.at[k - 1, j], recv.at[k - 1, j], at.along_a(k))
+            remote(src, dst, send.at[h, k - 1, j], recv.at[h, k - 1, j], at.along_a(k))
+            for h in (0, 1)
             for k in (1, 2, 3)
             for j in range(4)
         ]
-        local = [pltpu.make_async_copy(full.at[0, :, 0:half], buf.at[mine, 0:half], near.at[j]) for j in range(4)]
+        local = [pltpu.make_async_copy(src, dst, near.at[h, j]) for h in (0, 1) for j in range(4)]
         return far, local
 
     def shard_rows(s):
@@ -191,15 +245,18 @@
         term = jnp.dot(cot_full[s], wo[shard_rows(s), :], preferred_element_type=F32)
         d_heads[...] = term if first else d_heads[...] + term
 
+    def spread_cot(s, h):
+        spread_slab(cot_full, s, h, cot_a, cs, cr, cl)
+
     add_heads(m, True)
-    cots.arrive_other(0)
+    cots.near(0)
+    cots.other(0, 0)
+    cots.other(0, 1)
     add_heads(cots.others(0))
-    cots.arrive(1)
-    cots.arrive(3)
-    for k in (1, 3):
-        add_heads(cots.mine(k))
-        cots.arrive_other(k)
-        add_heads(cots.others(k))
+    cots.near(1)
+    cots.far(0)
+    add_heads(cots.mine(1))
+    add_heads(cots.mine(3))
 
     for copy in routes:
         copy.wait()
@@ -219,9 +276,14 @@
     for copy in stats:
         copy.start()
 
-    for k in (0, 1, 3):
-        spread_slab(cot_full, cots.mine(k), cot_a, cs, cr, cl)
-        spread_slab(cot_full, cots.others(k), cot_a, cs, cr, cl)
+    for h in (0, 1):
+        spread_cot(m, h)
+        spread_cot(cots.others(0), h)
+        for k in (1, 3):
+            spread_cot(cots.mine(k), h)
+            cots.other(k, h)
+            spread_cot(cots.others(k), h)
+    spread_cot(cots.mine(2), 0)
     for copy in stats:
         copy.wait()
     parts = [st_out[...]] + [st_in[k] for k in range(7)]
@@ -236,35 +298,55 @@
     norms = Collect(normed_full, nz, nzr, nb, nbr)
     norms.start()
 
-    cots.arrive(2)
-    spread_slab(cot_full, cots.mine(2), cot_a, cs, cr, cl)
-    add_heads(cots.mine(2))
-    cots.arrive_other(2)
-    spread_slab(cot_full, cots.others(2), cot_a, cs, cr, cl)
-    add_heads(cots.others(2))
-    load_wq.wait()
+    def spread_normed(s, h):
+        spread_slab(normed_full, s, h, normed_a, ns, nr, nl)
 
     def add_projected(s, first=False):
-        spread_slab(normed_full, s, normed_a, ns, nr, nl)
         for t in range(3):
             cols = slice(t * half, (t + 1) * half)
             term = jnp.dot(normed_full[s], wq[t, shard_rows(s), :], preferred_element_type=F32)
             proj[:, cols] = term if first else proj[:, cols] + term
 
+    cots.far(1)
+    spread_cot(cots.mine(2), 1)
+    for h in (0, 1):
+        cots.other(2, h)
+        spread_cot(cots.others(2), h)
+    for h in (0, 1):
+        spread_normed(m, h)
+    norms.near(0)
+    for k in (1, 3):
+        spread_normed(norms.mine(k), 0)
+    for h in (0, 1):
+        norms.other(0, h)
+        spread_normed(norms.others(0), h)
+    load_wq.wait()
     add_projected(m, True)
-    norms.arrive_other(0)
     add_projected(norms.others(0))
-    norms.arrive(1)
-    norms.arrive(3)
     for k in (1, 3):
+        norms.other(k, 0)
+        spread_normed(norms.others(k), 0)
+    for s in (cots.others(1), cots.others(3), cots.mine(2), cots.others(2)):
+        add_heads(s)
+    norms.near(1)
+    norms.far(0)
+    spread_normed(norms.mine(2), 0)
+    for k in (1, 3):
+        spread_normed(norms.mine(k), 1)
         add_projected(norms.mine(k))
-        norms.arrive_other(k)
+    norms.other(2, 0)
+    spread_normed(norms.others(2), 0)
+    for k in (1, 3):
+        norms.other(k, 1)
+        spread_normed(norms.others(k), 1)
+    for k in (1, 3):
         add_projected(norms.others(k))
-    norms.arrive(2)
+    norms.far(1)
+    spread_normed(norms.mine(2), 1)
+    norms.other(2, 1)
+    spread_normed(norms.others(2), 1)
     add_projected(norms.mine(2))
-    norms.arrive_other(2)
     add_projected(norms.others(2))
-
     same = places[:, 1:2] == segment[...].astype(F32)
 
     def normalise(values):
@@ -337,35 +419,13 @@
 
     sums = []
     for part in range(4):
-        far, after, ahead = (wo.at[held(part, i), :] for i in range(3))
-        pairs = [
-            (far.at[low, :], far_in.at[part, low, :], 1),
-            (far.at[high, :], far_in.at[part, high, :], 3),
-            (after, near_in.at[part, 0], 1),
-            (ahead, near_in.at[part, 1], 3),
-        ]
-        sums.append([remote(src, dst, qs.at[part, i], qr.at[part, i], at.along_b(to)) for i, (src, dst, to) in enumerate(pairs)])
-
-    def send_far(part):
-        wo[held(part, 0), :] = product(part, 2).astype(BF16)
-        sums[part][0].start()
-        sums[part][1].start()
-
-    def send_near(part):
-        for i, k in enumerate((1, 3)):
-            own_part[part] = product(part, k)
-            sums[part][i].wait_recv()
-            lines = (low, high)[i]
-            own_part[part, lines, :] += far_in[part, lines, :].astype(F32)
-            wo[held(part, 1 + i), :] = own_part[part].astype(BF16)
-            sums[part][2 + i].start()
-        own_part[part] = product(part, 0)
-
-    def total_of(part):
-        for i in (2, 3):
-            sums[part][i].wait_recv()
-        total = own_part[part] + near_in[part, 0].astype(F32) + near_in[part, 1].astype(F32)
-        return (total * scale).T.astype(BF16)
+        out = [wo.at[held(part, i), :] for i in range(3)]
+        sums.append(
+            Ring(
+                functools.partial(product, part), out, own_part.at[part], far_in.at[part], near_in.at[part],
+                qs.at[part], qr.at[part], at.along_b,
+            )
+        )
 
     cots.finish()
     cot_far, cot_near = spread_ends(cot_full, cot_a, cs, cr, cl)
@@ -374,72 +434,66 @@
     for copy in cot_near:
         copy.wait()
 
-    sib_out, z_out = cot_full.at[0:4], cot_full.at[4:7]
     def attn_term(shard):
-        rows = shard_rows(shard)
-        return nt_dot(heads[...], wo[rows, :])
+        return nt_dot(heads[...], wo[shard_rows(shard), :])
 
     def dn_term(shard):
-        rows = shard_rows(shard)
-        total = nt_dot(dproj[:, 0:half], wq[0, rows, :])
-        total += nt_dot(dproj[:, half : 2 * half], wq[1, rows, :])
-        return total + nt_dot(dproj[:, 2 * half : 3 * half], wq[2, rows, :])
-
-    def to_sibling(term, out, into, send, recv):
-        def step(k, carry):
-            out[k] = term(((z + 1 + k) % 4) * 2 + 1 - c).astype(BF16)
-            remote(out.at[k], into.at[k], send.at[k], recv.at[k], at.sibling()).start()
-            return carry
-
-        lax.fori_loop(0, 4, step, 0)
-
-    def along_z(term, sib_o, sib, sib_send, sib_recv, out, into, send, recv, own):
-        def step(k, carry):
-            value = term(((z + 1 + k) % 4) * 2 + c)
-            remote(sib_o.at[k], sib.at[k], sib_send.at[k], sib_recv.at[k], at.sibling()).wait()
-            out[k] = (value + sib[k].astype(F32)).astype(BF16)
-            remote(out.at[k], into.at[k], send.at[k], recv.at[k], at.along_z(1 + k)).start()
-            return carry
-
-        lax.fori_loop(0, 3, step, 0)
-        value = term(z * 2 + c)
-        remote(sib_o.at[3], sib.at[3], sib_send.at[3], sib_recv.at[3], at.sibling()).wait()
-        own[...] = value + sib[3].astype(F32)
-
-    to_sibling(attn_term, sib_out, sib_in, ss, sr)
+        total = nt_dot(dproj[:, 0:half], wq[0, shard_rows(shard), :])
+        total += nt_dot(dproj[:, half : 2 * half], wq[1, shard_rows(shard), :])
+        return total + nt_dot(dproj[:, 2 * half : 3 * half], wq[2, shard_rows(shard), :])
+
+    class ChipSum:
+        def __init__(self, term, out, into, send, recv):
+            self.term, self.out, self.into = term, out, into
+            self.copies = [remote(out.at[k], into.at[k], send.at[k], recv.at[k], at.sibling()) for k in range(4)]
+
+        def start(self):
+            for k in (2, 1, 3, 0):
+                self.out[k] = self.term(((z + k) % 4) * 2 + 1 - c).astype(BF16)
+                self.copies[k].start()
+
+        def sum(self, k):
+            value = self.term(((z + k) % 4) * 2 + c)
+            self.copies[k].wait()
+            return value + self.into[k].astype(F32)
+
+    attn_chip = ChipSum(attn_term, cot_full.at[0:4], sib_in, ss, sr)
+    dn_chip = ChipSum(dn_term, dn_sib_out, dn_sib_in, dss, dsr)
+    attn_out = [cot_full.at[4 + i] for i in range(3)]
+    dn_out = [dn_z_out.at[i] for i in range(3)]
+    attn_ring = Ring(attn_chip.sum, attn_out, own_at, z_in.at[0], z_in.at[1:3], zs, zr, at.along_z)
+    dn_ring = Ring(dn_chip.sum, dn_out, own_dn, dn_z_in.at[0], dn_z_in.at[1:3], dzs, dzr, at.along_z)
+
+    attn_chip.start()
+    dn_chip.start()
+    attn_ring.send_far()
+    attn_ring.send_near()
+    dn_ring.send_far()
     relay(0)
-    to_sibling(dn_term, dn_sib_out, dn_sib_in, dss, dsr)
     relay(1)
-    along_z(attn_term, sib_out, sib_in, ss, sr, z_out, z_in, zs, zr, own_at)
+    dn_ring.send_near()
+    relay(2)
+    relay(3)
     for copy in cot_far:
         copy.wait_recv()
     gathered(0)
-    send_far(0)
-    relay(2)
-    along_z(dn_term, dn_sib_out, dn_sib_in, dss, dsr, dn_z_out, dn_z_in, dzs, dzr, own_dn)
-    relay(3)
-    send_near(0)
+    sums[0].send_far()
     norms.finish()
     normed_far, normed_near = spread_ends(normed_full, normed_a, ns, nr, nl)
     for copy in normed_far + normed_near:
         copy.wait()
     for part in (1, 2, 3):
         gathered(part)
-        send_far(part)
-        if part > 1:
-            send_near(part - 1)
-    send_near(3)
-
-    total = own_at[...]
-    for k in range(3):
-        remote(z_out.at[k], z_in.at[k], zs.at[k], zr.at[k], at.along_z(1 + k)).wait()
-        total += z_in[k].astype(F32)
-    output[...] = (packed[...].astype(F32) + total).astype(BF16)
-
-    total = own_dn[...]
-    for k in range(3):
-        remote(dn_z_out.at[k], dn_z_in.at[k], dzs.at[k], dzr.at[k], at.along_z(1 + k)).wait()
-        total += dn_z_in[k].astype(F32)
+        sums[part].send_far()
+        sums[part - 1].send_near()
+    sums[3].send_near()
+
+    stores = [pltpu.make_async_copy(output, output_to, osem.at[0]), pltpu.make_async_copy(input_grad, input_grad_to, osem.at[1])]
+    stores.append(pltpu.make_async_copy(out_grad, out_grad_to, osem.at[2]))
+    stores += [pltpu.make_async_copy(qkv_grad.at[t], qkv_grad_to.at[t], osem.at[3 + t]) for t in range(3)]
+    output[...] = (packed[...].astype(F32) + attn_ring.total()).astype(BF16)
+    stores[0].start()
+    total = dn_ring.total()
     rstd = columns[:, 1:2]
     unit = (packed[...].astype(F32) - columns[:, 0:1]) * rstd
     u = total * gain_part
@@ -454,26 +508,37 @@
     unit = (packed[...].astype(F32) - columns[:, 0:1]) * rstd
     grad = rstd * (own_dn[...] - means[:, 0:1] - unit * means[:, 1:2])
     input_grad[...] = (cot[...].astype(F32) + grad).astype(BF16)
-
-    out_grad[...] = total_of(0)
-    for t in range(3):
-        qkv_grad[t] = total_of(1 + t)
+    stores[1].start()
     for part in range(4):
-        for copy in gathers[part] + sums[part]:
+        result = (sums[part].total() * scale).T.astype(BF16)
+        if part == 0:
+            out_grad[...] = result
+        else:
+            qkv_grad[part - 1] = result
+        stores[2 + part].start()
+    for ring in sums + [attn_ring, dn_ring]:
+        ring.finish()
+    for part in range(4):
+        for copy in gathers[part]:
             copy.wait_send()
+    for copy in stores:
+        copy.wait()
 
 
 def hand_over(*refs):
-    sources, results, sem = refs[:4], refs[4:8], refs[8]
-    copies = [pltpu.make_async_copy(src, dst, sem.at[i]) for i, (src, dst) in enumerate(zip(sources, results))]
-    for copy in copies:
+    sources, results, held, came, went = refs[:4], refs[4:8], refs[8:12], refs[12], refs[13]
+    ins = [pltpu.make_async_copy(src, buf, came.at[i]) for i, (src, buf) in enumerate(zip(sources, held))]
+    outs = [pltpu.make_async_copy(buf, dst, went.at[i]) for i, (buf, dst) in enumerate(zip(held, results))]
+    for copy in ins:
         copy.start()
-    for copy in copies:
+    for before, after in zip(ins, outs):
+        before.wait()
+        after.start()
+    for copy in outs:
         copy.wait()
 
 
 def shards(patches, dest_group, dest_row, segment, ln_gain, w_qkv, qk_gain, w_out, cotangent):
-    vmem = pl.BlockSpec(memory_space=pltpu.VMEM)
     anywhere = pl.BlockSpec(memory_space=pl.ANY)
     dma = pltpu.SemaphoreType.DMA
     V = pltpu.VMEM
@@ -487,9 +552,12 @@
     results = pl.pallas_call(
         functools.partial(whole, scale),
         out_shape=out_shape,
-        in_specs=[vmem, vmem, vmem, vmem, vmem, anywhere, vmem, anywhere, vmem],
-        out_specs=(vmem,) * 4,
+        in_specs=[anywhere] * 9,
+        out_specs=(anywhere,) * 4,
         scratch_shapes=[
+            V((256, 768), BF16), V((1, 256), jnp.int32), V((1, 256), jnp.int32), V((1, 256), jnp.int32),
+            V((1, 6144), F32), V((2, 128), F32), V((256, 768), BF16),
+            *(V(shape.shape, BF16) for shape in out_shape),
             V((512, 896), BF16), V((512, 896), BF16), V((256, 768), BF16),
             V((8, 256, 768), BF16), V((8, 256, 768), BF16),
             V((1024, 1536), BF16), V((1024, 1536), BF16), V((4, 384, 1024), BF16),
@@ -501,12 +569,12 @@
             V((4, 256, 768), BF16), V((4, 256, 768), BF16), V((3, 256, 768), BF16), V((3, 256, 768), BF16),
             V((4, 384, 384), BF16), V((4, 2, 384, 384), BF16),
             V((4, 384, 384), F32), V((256, 768), F32), V((256, 768), F32),
-            dma((2,)), dma((15,)), dma((15,)),
+            dma((8,)), dma((6,)), dma((2,)), dma((15,)), dma((15,)),
+            dma((2, 4)), dma((2, 4)), dma((2, 4)), dma((2, 4)), dma((2, 4)), dma((2, 4)), dma((2, 4)), dma((2, 4)),
+            dma((7,)), dma((7,)), dma((7,)), dma((7,)),
+            dma((2, 3, 4)), dma((2, 3, 4)), dma((2, 4)), dma((2, 3, 4)), dma((2, 3, 4)), dma((2, 4)),
+            dma((4, 4)), dma((4, 4)),
             dma((4,)), dma((4,)), dma((4,)), dma((4,)), dma((4,)), dma((4,)), dma((4,)), dma((4,)),
-            dma((7,)), dma((7,)), dma((7,)), dma((7,)),
-            dma((3, 4)), dma((3, 4)), dma((4,)), dma((3, 4)), dma((3, 4)), dma((4,)),
-            dma((4, 4)), dma((4, 4)),
-            dma((4,)), dma((4,)), dma((3,)), dma((3,)), dma((4,)), dma((4,)), dma((3,)), dma((3,)),
             dma((4, 4)), dma((4, 4)),
         ],
         compiler_params=pltpu.CompilerParams(
@@ -522,7 +590,7 @@
         out_shape=out_shape,
         in_specs=[anywhere] * 4,
         out_specs=(anywhere,) * 4,
-        scratch_shapes=[dma((4,))],
+        scratch_shapes=[V(shape.shape, BF16) for shape in out_shape] + [dma((4,)), dma((4,))],
         name="hand_over",
     )(*results)
     return (output, input_grad, jnp.transpose(qkv_grad, (1, 0, 2)), out_grad)

time: 172 us -> 113 us (0.66)
  Pallas kernels: 171 us -> 112 us
    pallas_call x1, Pallas kernels: 60.7 us -> 2.48 us  [shards(): pl.pallas_call(hand_over, out_shape=out_shape, in_specs=[anywhere] * 4, o...]
where the time goes in v4:
time: 113 us
  Pallas kernels  112 us (99%)
    pallas_call x1, Pallas kernels, shards(): pl.pallas_call(functools.partial(whole, scale), out_shape=out_shape, in_s...  110 us
    pallas_call x1, Pallas kernels, shards(): pl.pallas_call(hand_over, out_shape=out_shape, in_specs=[anywhere] * 4, o...  2.48 us

profile of v4, /device:TPU:1, one launch (start us, length us, event | category | flops | bytes accessed | tf_op | source)
XLA Modules:
  0.0 112.8 jit_solution(13543099080784883732)
XLA Ops:
  0.6 109.5 %whole.1 = (bf16[256,768]{1,0:T(8,128)(2,1)}, bf16[256,768]{1,0:T(8,128)(2,1)}, bf16[3,384,384]{2,1,0:T(8,128)(2,1)}, bf16[384,384]{1,0:T(8,128)(2,1)}) custom-call(bf16[256,768]{1,0:T(8,128)(2,1)} %patches_in.1, s32[1,256]{1,0:T(1,128)} %bitcast.8, s32[1,256]{1,0:T(1,128)} %bitcast.9, s32[1,256]{1,0:T(1,128)} %bitcast.10, f32[1,6144]{1,0:T(1,128)} %bitcast.7, ...), custom_call_target="tpu_custom_call" | custom-call | tf_op jit(solution)/shard_map/whole/pallas_call | solution.py:552
  110.2 2.5 %hand_over.1 = (bf16[256,768]{1,0:T(8,128)(2,1)}, bf16[256,768]{1,0:T(8,128)(2,1)}, bf16[3,384,384]{2,1,0:T(8,128)(2,1)}, bf16[384,384]{1,0:T(8,128)(2,1)}) custom-call(bf16[256,768]{1,0:T(8,128)(2,1)} %get-tuple-element.12.refs_0_, bf16[256,768]{1,0:T(8,128)(2,1)} %get-tuple-element.13.refs_1_, bf16[3,384,384]{2,1,0:T(8,128)(2,1)} %get-tuple-element.14.refs_2_, ...), custom_call_target="tpu_custom_call" | custom-call | tf_op jit(solution)/shard_map/hand_over/pallas_call | solution.py:588

commit v5 on v4

--- a/solution.py
+++ b/solution.py
@@ -107,7 +107,7 @@
     patches, dest_group, dest_row, segment, gain, qk_gain, cot, output, input_grad, qkv_grad, out_grad,
     outbox, inbox, packed, cot_full, normed_full, cot_a, normed_a, parts_a, wq, wo,
     proj, d_heads, heads, dproj, columns, places, st_pad, st_out, st_in, en_out, en_in,
-    sib_in, z_in, dn_sib_out, dn_sib_in, dn_z_out, dn_z_in, far_in, near_in,
+    sib_out, sib_in, z_out, z_in, dn_sib_out, dn_sib_in, dn_z_out, dn_z_in, far_in, near_in,
     own_part, own_at, own_dn,
     isem, osem, wsem, rs, rr, cz, czr, cb, cbr, nz, nzr, nb, nbr, sts, str_, ens, enr,
     cs, cr, cl, ns, nr, nl, gs, gr, ss, sr, zs, zr, dss, dsr, dzs, dzr, qs, qr,
@@ -393,21 +393,17 @@
     low, high, every = slice(0, 192), slice(192, 384), slice(0, 384)
     gathers = []
     for part in range(4):
-        hops = [(0, every, 1), (0, every, 3), (3, low, 1), (1, high, 3)]
+        hops = [(0, every, 1), (0, every, 3), (0, every, 2)]
         refs = [(window(part, k, lines), at.along_a(to)) for k, lines, to in hops]
         gathers.append([remote(src, src, gs.at[part, i], gr.at[part, i], to) for i, (src, to) in enumerate(refs)])
     for part in range(4):
         gathers[part][0].start()
         gathers[part][1].start()
-
-    def relay(part):
-        for i in (0, 1):
-            gathers[part][i].wait_recv()
-            gathers[part][i + 2].start()
+        gathers[part][2].start()
 
     def gathered(part):
-        gathers[part][2].wait_recv()
-        gathers[part][3].wait_recv()
+        for copy in gathers[part]:
+            copy.wait_recv()
 
     def held(part, i):
         return slice((3 * part + i) * half, (3 * part + i + 1) * half)
@@ -427,20 +423,15 @@
             )
         )
 
-    cots.finish()
     cot_far, cot_near = spread_ends(cot_full, cot_a, cs, cr, cl)
-    for copy in cot_far:
-        copy.wait_send()
-    for copy in cot_near:
-        copy.wait()
 
     def attn_term(shard):
-        return nt_dot(heads[...], wo[shard_rows(shard), :])
+        return jnp.dot(wo[shard_rows(shard), :], parts_a[0, :, mine], preferred_element_type=F32)
 
     def dn_term(shard):
-        total = nt_dot(dproj[:, 0:half], wq[0, shard_rows(shard), :])
-        total += nt_dot(dproj[:, half : 2 * half], wq[1, shard_rows(shard), :])
-        return total + nt_dot(dproj[:, 2 * half : 3 * half], wq[2, shard_rows(shard), :])
+        rows_of = shard_rows(shard)
+        terms = (jnp.dot(wq[t, rows_of, :], parts_a[t + 1, :, mine], preferred_element_type=F32) for t in range(3))
+        return sum(terms)
 
     class ChipSum:
         def __init__(self, term, out, into, send, recv):
@@ -457,9 +448,9 @@
             self.copies[k].wait()
             return value + self.into[k].astype(F32)
 
-    attn_chip = ChipSum(attn_term, cot_full.at[0:4], sib_in, ss, sr)
+    attn_chip = ChipSum(attn_term, sib_out, sib_in, ss, sr)
     dn_chip = ChipSum(dn_term, dn_sib_out, dn_sib_in, dss, dsr)
-    attn_out = [cot_full.at[4 + i] for i in range(3)]
+    attn_out = [z_out.at[i] for i in range(3)]
     dn_out = [dn_z_out.at[i] for i in range(3)]
     attn_ring = Ring(attn_chip.sum, attn_out, own_at, z_in.at[0], z_in.at[1:3], zs, zr, at.along_z)
     dn_ring = Ring(dn_chip.sum, dn_out, own_dn, dn_z_in.at[0], dn_z_in.at[1:3], dzs, dzr, at.along_z)
@@ -467,15 +458,12 @@
     attn_chip.start()
     dn_chip.start()
     attn_ring.send_far()
+    dn_ring.send_far()
     attn_ring.send_near()
-    dn_ring.send_far()
-    relay(0)
-    relay(1)
     dn_ring.send_near()
-    relay(2)
-    relay(3)
-    for copy in cot_far:
-        copy.wait_recv()
+    cots.finish()
+    for copy in cot_far + cot_near:
+        copy.wait()
     gathered(0)
     sums[0].send_far()
     norms.finish()
@@ -491,13 +479,13 @@
     stores = [pltpu.make_async_copy(output, output_to, osem.at[0]), pltpu.make_async_copy(input_grad, input_grad_to, osem.at[1])]
     stores.append(pltpu.make_async_copy(out_grad, out_grad_to, osem.at[2]))
     stores += [pltpu.make_async_copy(qkv_grad.at[t], qkv_grad_to.at[t], osem.at[3 + t]) for t in range(3)]
-    output[...] = (packed[...].astype(F32) + attn_ring.total()).astype(BF16)
+    output[...] = (packed[...].astype(F32) + attn_ring.total().T).astype(BF16)
     stores[0].start()
-    total = dn_ring.total()
+    total = dn_ring.total().T
     rstd = columns[:, 1:2]
     unit = (packed[...].astype(F32) - columns[:, 0:1]) * rstd
     u = total * gain_part
-    own_dn[...] = u
+    proj[:, 0:width] = u
     ends = exchange(jnp.sum(u, -1, keepdims=True), jnp.sum(u * unit, -1, keepdims=True), en_out, en_in, ens, enr)
     for copy in ends:
         copy.start()
@@ -506,7 +494,7 @@
     st_pad[0:8, :] = (en_out[...] + sum(en_in[k] for k in range(7))) * (1.0 / 6144.0)
     means = st_pad[...].T
     unit = (packed[...].astype(F32) - columns[:, 0:1]) * rstd
-    grad = rstd * (own_dn[...] - means[:, 0:1] - unit * means[:, 1:2])
+    grad = rstd * (proj[:, 0:width] - means[:, 0:1] - unit * means[:, 1:2])
     input_grad[...] = (cot[...].astype(F32) + grad).astype(BF16)
     stores[1].start()
     for part in range(4):
@@ -565,10 +553,10 @@
             V((256, 1152), F32), V((256, 384), F32), V((256, 384), BF16), V((256, 1152), BF16),
             V((256, 128), F32), V((256, 128), F32), V((128, 256), F32),
             V((8, 256), F32), V((7, 8, 256), F32), V((8, 256), F32), V((7, 8, 256), F32),
-            V((4, 256, 768), BF16), V((3, 256, 768), BF16),
-            V((4, 256, 768), BF16), V((4, 256, 768), BF16), V((3, 256, 768), BF16), V((3, 256, 768), BF16),
+            V((4, 768, 256), BF16), V((4, 768, 256), BF16), V((3, 768, 256), BF16), V((3, 768, 256), BF16),
+            V((4, 768, 256), BF16), V((4, 768, 256), BF16), V((3, 768, 256), BF16), V((3, 768, 256), BF16),
             V((4, 384, 384), BF16), V((4, 2, 384, 384), BF16),
-            V((4, 384, 384), F32), V((256, 768), F32), V((256, 768), F32),
+            V((4, 384, 384), F32), V((768, 256), F32), V((768, 256), F32),
             dma((8,)), dma((6,)), dma((2,)), dma((15,)), dma((15,)),
             dma((2, 4)), dma((2, 4)), dma((2, 4)), dma((2, 4)), dma((2, 4)), dma((2, 4)), dma((2, 4)), dma((2, 4)),
             dma((7,)), dma((7,)), dma((7,)), dma((7,)),

time: 113 us -> 106 us (0.938)
  Pallas kernels: 112 us -> 105 us
    pallas_call x1, Pallas kernels: 110 us -> 102 us  [shards(): pl.pallas_call(functools.partial(whole, scale), out_shape=out_shape, in_s...]
where the time goes in v5:
time: 106 us
  Pallas kernels  105 us (99%)
    pallas_call x1, Pallas kernels, shards(): pl.pallas_call(functools.partial(whole, scale), out_shape=out_shape, in_s...  102 us
    pallas_call x1, Pallas kernels, shards(): pl.pallas_call(hand_over, out_shape=out_shape, in_specs=[anywhere] * 4, o...  2.48 us

profile of v5, /device:TPU:1, one launch (start us, length us, event | category | flops | bytes accessed | tf_op | source)
XLA Modules:
  0.0 105.5 jit_solution(13149665966326125141)
XLA Ops:
  0.6 102.2 %whole.1 = (bf16[256,768]{1,0:T(8,128)(2,1)}, bf16[256,768]{1,0:T(8,128)(2,1)}, bf16[3,384,384]{2,1,0:T(8,128)(2,1)}, bf16[384,384]{1,0:T(8,128)(2,1)}) custom-call(bf16[256,768]{1,0:T(8,128)(2,1)} %patches_in.1, s32[1,256]{1,0:T(1,128)} %bitcast.8, s32[1,256]{1,0:T(1,128)} %bitcast.9, s32[1,256]{1,0:T(1,128)} %bitcast.10, f32[1,6144]{1,0:T(1,128)} %bitcast.7, ...), custom_call_target="tpu_custom_call" | custom-call | tf_op jit(solution)/shard_map/whole/pallas_call | solution.py:540
  102.9 2.5 %hand_over.1 = (bf16[256,768]{1,0:T(8,128)(2,1)}, bf16[256,768]{1,0:T(8,128)(2,1)}, bf16[3,384,384]{2,1,0:T(8,128)(2,1)}, bf16[384,384]{1,0:T(8,128)(2,1)}) custom-call(bf16[256,768]{1,0:T(8,128)(2,1)} %get-tuple-element.12.refs_0_, bf16[256,768]{1,0:T(8,128)(2,1)} %get-tuple-element.13.refs_1_, bf16[3,384,384]{2,1,0:T(8,128)(2,1)} %get-tuple-element.14.refs_2_, ...), custom_call_target="tpu_custom_call" | custom-call | tf_op jit(solution)/shard_map/hand_over/pallas_call | solution.py:576

commit v6 on v5

--- a/solution.py
+++ b/solution.py
@@ -470,10 +470,12 @@
     normed_far, normed_near = spread_ends(normed_full, normed_a, ns, nr, nl)
     for copy in normed_far + normed_near:
         copy.wait()
+    sums[0].send_near()
     for part in (1, 2, 3):
         gathered(part)
         sums[part].send_far()
-        sums[part - 1].send_near()
+    sums[1].send_near()
+    sums[2].send_near()
     sums[3].send_near()
 
     stores = [pltpu.make_async_copy(output, output_to, osem.at[0]), pltpu.make_async_copy(input_grad, input_grad_to, osem.at[1])]

time: 106 us -> 105 us (level)
  no operation moved by 1% of the time
where the time goes in v6:
time: 105 us
  Pallas kernels  104 us (99%)
    pallas_call x1, Pallas kernels, shards(): pl.pallas_call(functools.partial(whole, scale), out_shape=out_shape, in_s...  102 us
    pallas_call x1, Pallas kernels, shards(): pl.pallas_call(hand_over, out_shape=out_shape, in_specs=[anywhere] * 4, o...  2.48 us

profile of v6, /device:TPU:1, one launch (start us, length us, event | category | flops | bytes accessed | tf_op | source)
XLA Modules:
  0.0 105.1 jit_solution(5397511083989870003)
XLA Ops:
  0.6 101.8 %whole.1 = (bf16[256,768]{1,0:T(8,128)(2,1)}, bf16[256,768]{1,0:T(8,128)(2,1)}, bf16[3,384,384]{2,1,0:T(8,128)(2,1)}, bf16[384,384]{1,0:T(8,128)(2,1)}) custom-call(bf16[256,768]{1,0:T(8,128)(2,1)} %patches_in.1, s32[1,256]{1,0:T(1,128)} %bitcast.8, s32[1,256]{1,0:T(1,128)} %bitcast.9, s32[1,256]{1,0:T(1,128)} %bitcast.10, f32[1,6144]{1,0:T(1,128)} %bitcast.7, ...), custom_call_target="tpu_custom_call" | custom-call | tf_op jit(solution)/shard_map/whole/pallas_call | solution.py:542
  102.5 2.5 %hand_over.1 = (bf16[256,768]{1,0:T(8,128)(2,1)}, bf16[256,768]{1,0:T(8,128)(2,1)}, bf16[3,384,384]{2,1,0:T(8,128)(2,1)}, bf16[384,384]{1,0:T(8,128)(2,1)}) custom-call(bf16[256,768]{1,0:T(8,128)(2,1)} %get-tuple-element.12.refs_0_, bf16[256,768]{1,0:T(8,128)(2,1)} %get-tuple-element.13.refs_1_, bf16[3,384,384]{2,1,0:T(8,128)(2,1)} %get-tuple-element.14.refs_2_, ...), custom_call_target="tpu_custom_call" | custom-call | tf_op jit(solution)/shard_map/hand_over/pallas_call | solution.py:578

commit v7 on v6

--- a/solution.py
+++ b/solution.py
@@ -254,7 +254,6 @@
     cots.other(0, 1)
     add_heads(cots.others(0))
     cots.near(1)
-    cots.far(0)
     add_heads(cots.mine(1))
     add_heads(cots.mine(3))
 
@@ -283,6 +282,7 @@
             spread_cot(cots.mine(k), h)
             cots.other(k, h)
             spread_cot(cots.others(k), h)
+    cots.far(0)
     spread_cot(cots.mine(2), 0)
     for copy in stats:
         copy.wait()

time: 105 us -> 105 us (level)
  no operation moved by 1% of the time
where the time goes in v7:
time: 105 us; the launch traced here: 104 us
  Pallas kernels  104 us (99%)
    pallas_call x1, Pallas kernels, shards(): pl.pallas_call(functools.partial(whole, scale), out_shape=out_shape, in_s...  101 us
    pallas_call x1, Pallas kernels, shards(): pl.pallas_call(hand_over, out_shape=out_shape, in_specs=[anywhere] * 4, o...  2.48 us

profile of v7, /device:TPU:1, one launch (start us, length us, event | category | flops | bytes accessed | tf_op | source)
XLA Modules:
  0.0 104.4 jit_solution(17767445216225799392)
XLA Ops:
  0.6 101.1 %whole.1 = (bf16[256,768]{1,0:T(8,128)(2,1)}, bf16[256,768]{1,0:T(8,128)(2,1)}, bf16[3,384,384]{2,1,0:T(8,128)(2,1)}, bf16[384,384]{1,0:T(8,128)(2,1)}) custom-call(bf16[256,768]{1,0:T(8,128)(2,1)} %patches_in.1, s32[1,256]{1,0:T(1,128)} %bitcast.8, s32[1,256]{1,0:T(1,128)} %bitcast.9, s32[1,256]{1,0:T(1,128)} %bitcast.10, f32[1,6144]{1,0:T(1,128)} %bitcast.7, ...), custom_call_target="tpu_custom_call" | custom-call | tf_op jit(solution)/shard_map/whole/pallas_call | solution.py:542
  101.8 2.5 %hand_over.1 = (bf16[256,768]{1,0:T(8,128)(2,1)}, bf16[256,768]{1,0:T(8,128)(2,1)}, bf16[3,384,384]{2,1,0:T(8,128)(2,1)}, bf16[384,384]{1,0:T(8,128)(2,1)}) custom-call(bf16[256,768]{1,0:T(8,128)(2,1)} %get-tuple-element.12.refs_0_, bf16[256,768]{1,0:T(8,128)(2,1)} %get-tuple-element.13.refs_1_, bf16[3,384,384]{2,1,0:T(8,128)(2,1)} %get-tuple-element.14.refs_2_, ...), custom_call_target="tpu_custom_call" | custom-call | tf_op jit(solution)/shard_map/hand_over/pallas_call | solution.py:578
